TPU v7x, 512 devices: a whole 4x8x8 slice. The times are simulated.
512 devices in a mesh: head: 8 (over y_lo, x), seq: 64 (over y_hi, z, core).
Axes of the slice: x: 4, y: 8 (y_hi: 4, y_lo: 2; y = y_hi * 2 + y_lo), z: 8, core: 2. Of those that a mesh axis runs over, the one named last changes fastest.
Arguments:
- queries: bfloat16 [2, 4096, 4096], P(None, 'seq', 'head'), may hold values from -256 to 256
- keys: bfloat16 [2, 4096, 4096], P(None, 'seq', 'head'), may hold values from -256 to 256
- values: bfloat16 [2, 4096, 4096], P(None, 'seq', 'head'), may hold values from -6 to 6
- token_rates: float32 [1, 16, 4096], P(None, 'head', 'seq'), may hold values from 0.1 to 1
- step_size: float32 [16], P('head'), may hold values from 0.3 to 1
- w_gate: bfloat16 [16, 256, 512], P('head', 'seq'), may hold values from -0.375 to 0.375
- w_up: bfloat16 [16, 256, 512], P('head', 'seq'), may hold values from -0.375 to 0.375
- w_down: bfloat16 [16, 512, 256], P('head', 'seq'), may hold values from -0.25 to 0.25
- norm_gain: float32 [4096], replicated, may hold values from 0.5 to 1.5
Outputs:
- mixed: bfloat16 [2, 4096, 4096], P(None, ('seq', 'head'))
All inputs are finite; a program needn't handle non-finite values.
Results may differ from a plain program's by a relative error of at most 0.0095.
Values may be sent and summed in bfloat16 or wider, within the bound.
No kernel may reach another device: no remote copies, remote signals or barrier semaphores. Data moves between devices by JAX's collectives and lax.ppermute only.
A program may use at most 64 MiB of HBM per device.

v0:
```python
import math

import jax
import jax.numpy as jnp
from jax import lax
from jax.experimental import pallas as pl
from jax.experimental.pallas import tpu as pltpu
from jax.sharding import Mesh
from jax.sharding import PartitionSpec as P

DH = 256
DF = 512
PART = 128
NS_STEPS = 5
CHIPS = 32
TOK = 128
REACH = 4
RING = ("y_hi", "z")
F32 = jnp.float32
BF = jnp.bfloat16


def matmul(left, right):
    return lax.dot_general(left, right, (((1,), (0,)), ((), ())), preferred_element_type=F32)


def matmul_nt(left, right):
    return lax.dot_general(left, right, (((1,), (1,)), ((), ())), preferred_element_type=F32)


def matmul_tn(left, right):
    return lax.dot_general(left, right, (((0,), (0,)), ((), ())), preferred_element_type=F32)


def halves(wide):
    high = wide.astype(BF)
    return high, (wide - high.astype(F32)).astype(BF)


def rms_norm(values_in):
    wide = values_in.astype(F32)
    mean_square = jnp.mean(wide * wide, axis=-1, keepdims=True)
    return (wide * lax.rsqrt(mean_square + 1e-06)).astype(BF)


def sigmoid(value):
    return 1.0 / (1.0 + jnp.exp(-value))


def fast_forward(query, gate_fast, up_fast, down_fast):
    query_norm = rms_norm(query)
    gate_query = matmul(query_norm, gate_fast)
    up_query = matmul(query_norm, up_fast)
    hidden = (gate_query * sigmoid(gate_query) * up_query).astype(BF)
    return matmul(hidden, down_fast)


def pack_kernel(
    core_ref, q_in, k_in, v_in, rate_in, gate_in, up_in, down_in, mine_ref, other_ref, deal_ref, *scratch
):
    sources = (q_in, k_in, v_in, rate_in, gate_in, up_in, down_in)
    q_ref, k_ref, v_ref, rate_ref, gate_ref, up_ref, down_ref = scratch[:7]
    semaphores = scratch[7]
    copies = [
        pltpu.make_async_copy(source, target, semaphores.at[index])
        for index, (source, target) in enumerate(zip(sources, scratch[:7]))
    ]
    for copy in copies:
        copy.start()
    for copy in copies:
        copy.wait()

    def fill(target, head):
        columns = slice(head * DH, (head + 1) * DH)
        for index, ref in enumerate((q_ref, k_ref, v_ref)):
            for block in range(2):
                first = (index * 2 + block) * 64
                target[first : first + 64, :] = ref[block, :, columns]
        rate = rate_ref[0, head : head + 1, :]
        high = rate.astype(BF).astype(F32)
        middle = (rate - high).astype(BF).astype(F32)
        low = (rate - high) - middle
        terms = jnp.concatenate([high, middle, low, jnp.zeros_like(rate)], 1)
        target[384:392, :] = jnp.broadcast_to(terms, (8, DH)).astype(BF)

    for head in range(2):

        @pl.when(core_ref[0] == head)
        def _():
            fill(mine_ref, head)
            fill(other_ref, 1 - head)

        tiles = []
        for ref in (gate_ref, up_ref):
            wide = ref[head].astype(F32)
            tiles += [wide[:, :DH], wide[:, DH:]]
        tiles.append(down_ref[head].astype(F32))
        piece = jnp.concatenate(tiles, 0).astype(BF)
        for row in range(4):
            deal_ref[row, 24 * head : 24 * head + 24, :] = piece


def regroup_kernel(rows_ref, deal_ref):
    for head in range(2):
        for row in range(4):
            piece = rows_ref[row, 24 * head : 24 * head + 24, :]
            for depth in range(8):
                deal_ref[2 * depth + head, 24 * row : 24 * row + 24, :] = piece


def arrange_kernel(core_ref, mine_ref, arrived_ref, own_ref, context_ref, pool_ref):
    own_ref[core_ref[0]] = mine_ref[...]
    own_ref[1 - core_ref[0]] = arrived_ref[...]
    for source in range(2):
        context_ref[source] = own_ref[source, 128:384, :]
        for index in range(2):
            first = 128 * index + 64 * source
            rows = slice(128 * (index + 1), 128 * (index + 1) + 64)
            pool_ref[first : first + 64, :] = own_ref[source, rows, :]
        pool_ref[256 + 8 * source : 264 + 8 * source, :] = own_ref[source, 384:392, :]


def grad_kernel(row_ref, p0_ref, p1_ref, p2_ref, p3_ref, raw_ref, grad_ref, slices_ref, down_ref):
    pools = (p0_ref, p1_ref, p2_ref, p3_ref)
    out_row = lax.broadcasted_iota(jnp.int32, (DH, 2 * DH), 0)
    in_row = lax.broadcasted_iota(jnp.int32, (DH, 2 * DH), 1)
    sender = out_row // 4
    pick = (sender % 16) * 32 + (sender // 16) * 8 + out_row % 4
    for index in range(2):
        first = 8 * index
        pieces = [raw_ref[:, 24 * y + first : 24 * y + first + 8, :].astype(F32) for y in range(4)]
        mixed = jnp.stack(pieces, 1).reshape(2 * DH, DH).astype(BF)
        rows = slice(index * DH, (index + 1) * DH)
        for half in range(2):
            chosen = jnp.where(in_row == pick + 4 * half, 1.0, 0.0).astype(BF)
            ordered = matmul(chosen, mixed).astype(BF)
            slices_ref[2 * half, rows, :] = ordered[:, :PART]
            slices_ref[2 * half + 1, rows, :] = ordered[:, PART:]
    for y in range(4):
        piece = raw_ref[:, 24 * y + 16 : 24 * y + 24, :].astype(F32).reshape(PART, DH)
        down_ref[PART * y : PART * (y + 1), :] = piece.astype(BF)
    row = row_ref[0]
    weights = (slices_ref[row, :DH, :], slices_ref[row, DH:, :])
    down_part = down_ref[pl.ds(pl.multiple_of(row * PART, PART), PART), :]
    equal = lax.broadcasted_iota(jnp.int32, (64, 64), 0) == lax.broadcasted_iota(
        jnp.int32, (64, 64), 1
    )
    columns = []
    for pool in pools:
        for source in range(2):
            terms = pool[256 + 8 * source : 264 + 8 * source, :].astype(F32)[0:1]
            rate = terms[:, 0:64] + (terms[:, 64:128] + terms[:, 128:192])
            spread = jnp.where(equal, jnp.broadcast_to(rate, (64, 64)), 0.0)
            columns.append(jnp.sum(spread, axis=1, keepdims=True))
    rate_col = jnp.concatenate(columns, 0)
    gate_part, up_part = weights
    keys_now = rms_norm(jnp.concatenate([pool[0:128, :] for pool in pools], 0))
    vals_now = jnp.concatenate([pool[128:256, :] for pool in pools], 0)
    gate_pre = matmul(keys_now, gate_part)
    up_pre = matmul(keys_now, up_part)
    back = matmul_nt(vals_now, down_part)
    sigmoid_val = sigmoid(gate_pre)
    act_val = gate_pre * sigmoid_val
    rate_back = rate_col * back
    d_gate = (rate_back * up_pre * sigmoid_val * (1.0 + gate_pre * (1.0 - sigmoid_val))).astype(BF)
    d_up = (rate_back * act_val).astype(BF)
    h_rate = (rate_col * act_val * up_pre).astype(BF)
    for index, (left, right) in enumerate(
        ((keys_now, d_gate), (keys_now, d_up), (vals_now, h_rate))
    ):
        grad = matmul_tn(left, right).reshape(8, 32, PART)
        grad_ref[:, index * 32 : index * 32 + 32, :] = grad.astype(BF)


def sum_kernel(parts_ref, total_ref):
    total = jnp.sum(parts_ref[...].astype(F32), axis=0, keepdims=True)
    total_ref[...] = jnp.broadcast_to(total, (8, 96, PART)).astype(BF)


def widen_kernel(piece_ref, total_ref):
    for row in range(4):
        total_ref[row] = piece_ref[...]


def whole_weights(slices_ref):
    gate_fast = jnp.concatenate([slices_ref[row, :DH, :] for row in range(4)], 1)
    up_fast = jnp.concatenate([slices_ref[row, DH:, :] for row in range(4)], 1)
    return gate_fast, up_fast


def attention_kernel(
    chip_ref, own_ref, c1_ref, c2_ref, c3_ref, c4_ref, slices_ref, down_ref, fast_ref, out_ref
):
    chip = chip_ref[0]
    row = lax.broadcasted_iota(jnp.int32, (TOK, TOK), 0)
    column = lax.broadcasted_iota(jnp.int32, (TOK, TOK), 1)
    scale = 1.0 / math.sqrt(DH)
    chunks = (c1_ref, c2_ref, c3_ref, c4_ref)

    def rows_of(distance, index, block):
        if distance == 0:
            first = (2 + 2 * index + block) * 64
            return jnp.concatenate([own_ref[src, first : first + 64, :] for src in range(2)], 0)
        behind = (chip < distance).astype(jnp.int32)
        place = 2 * index + jnp.maximum(block - behind, 0)
        chunk = chunks[distance - 1]
        return jnp.concatenate([chunk[0, place], chunk[1, place]], 0)

    for block in range(2):
        rows = slice(block * 64, block * 64 + 64)
        query = jnp.concatenate([own_ref[0, rows, :], own_ref[1, rows, :]], 0)
        scores = []
        for distance in range(REACH + 1):
            score = matmul_nt(query, rows_of(distance, 0, block)) * scale
            if distance == 0:
                score = jnp.where(row >= column, score, -1e30)
            elif distance == REACH:
                score = jnp.where(row < column, score, -1e30)
            if block == 0 and distance > 0:
                behind = (chip < distance).astype(jnp.int32)
                score = jnp.where(behind + jnp.zeros_like(row) > 0, -1e30, score)
            scores.append(score)
        top = scores[0]
        for score in scores[1:]:
            top = jnp.maximum(top, score)
        row_top = jnp.max(top, axis=-1, keepdims=True)
        exps = [jnp.exp(score - row_top) for score in scores]
        total = exps[0]
        for exp_score in exps[1:]:
            total = total + exp_score
        row_sum = jnp.sum(total, axis=-1, keepdims=True)
        result = None
        for distance in range(REACH + 1):
            weights = (exps[distance] / row_sum).astype(BF)
            part = matmul(weights, rows_of(distance, 1, block))
            result = part if result is None else result + part
        if block == 0:
            result = result + fast_forward(query, *whole_weights(slices_ref), down_ref[...])
        else:
            result = result + fast_ref[...]
        out_ref[:, block] = result.reshape(16, 8, DH).astype(BF)


def coarse_step(iterates):
    highs = [iterate.astype(BF) for iterate in iterates]
    grams = [matmul_nt(high, high) for high in highs]
    squares = [matmul(gram.astype(BF), gram.astype(BF)) for gram in grams]
    polys = [-4.775 * gram + 2.0315 * square for gram, square in zip(grams, squares)]
    changes = [matmul(poly.astype(BF), high) for poly, high in zip(polys, highs)]
    return [3.4445 * iterate + change for iterate, change in zip(iterates, changes)]


def thrice(left, right, axis):
    left = jnp.concatenate([left[0], left[0], left[1]], 1)
    return left, jnp.concatenate([right[0], right[1], right[0]], axis)


def fine_step(iterates):
    parts = [halves(iterate) for iterate in iterates]
    grams = [matmul_nt(*thrice(part, part, 1)) for part in parts]
    gram_parts = [halves(gram) for gram in grams]
    squares = [matmul(*thrice(part, part, 0)) for part in gram_parts]
    polys = [halves(-4.775 * gram + 2.0315 * square) for gram, square in zip(grams, squares)]
    changes = [matmul(*thrice(poly, part, 0)) for poly, part in zip(polys, parts)]
    return [3.4445 * iterate + change for iterate, change in zip(iterates, changes)]


def newton_kernel(
    step_ref, total_ref, slices_ref, down_ref, own_ref, _, fast_ref, iterate_ref
):
    for index in range(3):
        rows = slice(index * 32, index * 32 + 32)
        pieces = [total_ref[row, :, rows, :].astype(F32).reshape(DH, PART) for row in range(4)]
        grad = jnp.concatenate(pieces, 1)
        square = jnp.sum(jnp.sum(grad * grad, axis=0, keepdims=True), axis=1, keepdims=True)
        iterate_ref[index] = grad / (jnp.sqrt(square) + 1e-07)

    iterates = [iterate_ref[index] for index in range(3)]
    for step_index in range(NS_STEPS):
        iterates = coarse_step(iterates) if step_index < 2 else fine_step(iterates)
        for index in range(3):
            iterate_ref[index] = iterates[index]
        iterates = [iterate_ref[index] for index in range(3)]
    step = step_ref[0]
    gate_fast, up_fast = whole_weights(slices_ref)
    gate_fast = (gate_fast.astype(F32) + step * iterate_ref[0]).astype(BF)
    up_fast = (up_fast.astype(F32) + step * iterate_ref[1]).astype(BF)
    down_fast = (down_ref[...].astype(F32) + step * iterate_ref[2].T).astype(BF)
    query = jnp.concatenate([own_ref[0, 64:128, :], own_ref[1, 64:128, :]], 0)
    fast_ref[...] = fast_forward(query, gate_fast, up_fast, down_fast)


def norm_kernel(parts_ref, gain_ref, out_ref):
    square = None
    for source in range(16):
        wide = parts_ref[source].astype(F32)
        part = jnp.sum(wide * wide, axis=-1, keepdims=True)
        square = part if square is None else square + part
    scale = lax.rsqrt(square * (1.0 / (16 * DH)) + 1e-06)
    for source in range(16):
        head = 2 * (source % 8) + source // 8
        columns = slice(head * DH, (head + 1) * DH)
        wide = parts_ref[source].astype(F32) * scale * gain_ref[:, columns][None]
        out_ref[:, :, columns] = wide.astype(BF)


PARAMS = pltpu.CompilerParams(vmem_limit_bytes=16 * 1024 * 1024)
VMEM = pl.BlockSpec(memory_space=pltpu.VMEM)
ANY = pl.BlockSpec(memory_space=pl.ANY)
HBM = pl.BlockSpec(memory_space=pltpu.HBM)
SMEM = pl.BlockSpec(memory_space=pltpu.SMEM)


def shape_of(shape, dtype=BF):
    return jax.ShapeDtypeStruct(shape, dtype)


def body(queries, keys, values, token_rates, step_size, w_gate, w_up, w_down, norm_gain):
    core = lax.axis_index("core")
    chip = lax.axis_index(RING).astype(jnp.int32).reshape(1)
    line = lax.axis_index("y_hi").astype(jnp.int32).reshape(1)
    pieces = (queries, keys, values, token_rates, w_gate, w_up, w_down)
    place = core.astype(jnp.int32).reshape(1)
    mine, other, dealt = pl.pallas_call(
        pack_kernel,
        out_shape=(shape_of((392, DH)), shape_of((392, DH)), shape_of((4, 48, DH))),
        in_specs=[SMEM] + [HBM] * 7,
        out_specs=(VMEM,) * 3,
        scratch_shapes=[pltpu.VMEM(piece.shape, piece.dtype) for piece in pieces]
        + [pltpu.SemaphoreType.DMA((7,))],
        compiler_params=pltpu.CompilerParams(vmem_limit_bytes=61500 * 1024),
        name="pack",
    )(place, *pieces)
    dealt = lax.all_to_all(dealt, "y_hi", 0, 0, tiled=True)
    dealt = pl.pallas_call(
        regroup_kernel,
        out_shape=shape_of((16, 96, DH)),
        in_specs=[VMEM],
        out_specs=VMEM,
        compiler_params=PARAMS,
        name="regroup",
    )(dealt)
    dealt = lax.all_to_all(dealt, ("z", "core"), 0, 0, tiled=True)
    arrived = lax.ppermute(other, "core", [(0, 1), (1, 0)])
    own, context, pool = pl.pallas_call(
        arrange_kernel,
        out_shape=(shape_of((2, 392, DH)), shape_of((2, 256, DH)), shape_of((272, DH))),
        in_specs=[SMEM, VMEM, VMEM],
        out_specs=(VMEM,) * 3,
        compiler_params=PARAMS,
        name="arrange",
    )(place, mine, arrived)
    pools = [pool]
    for distance in range(1, 4):
        pools.append(lax.ppermute(pool, "y_hi", [(i, (i + distance) % 4) for i in range(4)]))
    ring = [(i, (i + 1) % CHIPS) for i in range(CHIPS)]
    chunks = [lax.ppermute(context, RING, ring)]

    grad, slices, down_fast = pl.pallas_call(
        grad_kernel,
        out_shape=(shape_of((8, 96, PART)), shape_of((4, 2 * DH, PART)), shape_of((DF, DH))),
        in_specs=[SMEM] + [VMEM] * 5,
        out_specs=(VMEM,) * 3,
        compiler_params=PARAMS,
        name="grad",
    )(line, *pools, dealt)
    parts = lax.all_to_all(grad, "z", 0, 0, tiled=True)
    chunks.append(lax.ppermute(chunks[-1], RING, ring))
    total = pl.pallas_call(
        sum_kernel,
        out_shape=shape_of((8, 96, PART)),
        in_specs=[VMEM],
        out_specs=VMEM,
        compiler_params=PARAMS,
        name="sum",
    )(parts)
    total = lax.all_to_all(total, "z", 0, 0, tiled=True)
    chunks.append(lax.ppermute(chunks[-1], RING, ring))
    total = pl.pallas_call(
        widen_kernel,
        out_shape=shape_of((4, 8, 96, PART)),
        in_specs=[VMEM],
        out_specs=VMEM,
        compiler_params=PARAMS,
        name="widen",
    )(total)
    total = lax.all_to_all(total, "y_hi", 0, 0, tiled=True)

    step = lax.dynamic_slice_in_dim(step_size, core, 1, 0)
    fast = pl.pallas_call(
        newton_kernel,
        out_shape=shape_of((TOK, DH), F32),
        in_specs=[SMEM] + [VMEM] * 4 + [ANY],
        out_specs=VMEM,
        scratch_shapes=[pltpu.VMEM((3, DH, DF), F32)],
        compiler_params=PARAMS,
        cost_estimate=pl.CostEstimate(
            flops=8_000_000_000, transcendentals=100_000, bytes_accessed=4_000_000
        ),
        name="newton",
    )(step, total, slices, down_fast, own, chunks[2])
    chunks.append(lax.ppermute(chunks[-1], RING, ring))
    chunks = [chunk.reshape(2, 4, 64, DH) for chunk in chunks]
    combined = pl.pallas_call(
        attention_kernel,
        out_shape=shape_of((16, 2, 8, DH)),
        in_specs=[SMEM] + [VMEM] * 8,
        out_specs=VMEM,
        compiler_params=PARAMS,
        name="window",
    )(chip, own, *chunks, slices, down_fast, fast)
    gathered = lax.all_to_all(combined, ("core", "y_lo", "x"), 0, 0, tiled=True)
    return pl.pallas_call(
        norm_kernel,
        out_shape=jax.ShapeDtypeStruct((2, 8, 16 * DH), BF),
        in_specs=[VMEM] * 2,
        out_specs=VMEM,
        compiler_params=PARAMS,
        name="norm",
    )(gathered, norm_gain.reshape(1, 16 * DH))


def solution(mesh):
    fine = Mesh(mesh.devices.reshape(2, 4, 4, 8, 2), ("y_lo", "x", "y_hi", "z", "core"))
    seq = RING + ("core",)
    head = ("y_lo", "x")
    placed = (
        P(None, seq, head),
        P(None, seq, head),
        P(None, seq, head),
        P(None, head, seq),
        P(head),
        P(head, seq, None),
        P(head, seq, None),
        P(head, seq, None),
        P(),
    )
    return jax.shard_map(
        body, mesh=fine, in_specs=placed, out_specs=P(None, seq + head, None), check_vma=False
    )
```

profile of v0, /device:TPU:1, one launch (start us, length us, event | category | flops | bytes accessed | tf_op | source)
XLA Modules:
  0.0 171.6 jit_solution(2386331206133159386)
XLA Ops:
  0.0 2.0 %pack.1 = (bf16[392,256]{1,0:T(8,128)(2,1)}, bf16[392,256]{1,0:T(8,128)(2,1)}, bf16[4,48,256]{2,1,0:T(8,128)(2,1)}) custom-call(s32[1]{0:T(128)} %bitcast.1.core_ref, bf16[2,64,512]{2,1,0:T(8,128)(2,1)} %q_in.1, bf16[2,64,512]{2,1,0:T(8,128)(2,1)} %k_in.1, bf16[2,64,512]{2,1,0:T(8,128)(2,1)} %v_in.1, f32[1,2,64]{2,1,0:T(2,128)} %rate_in.1, ...), custom_call_target="tpu_custom_call" | custom-call | tf_op jit(solution)/shard_map/pack/pallas_call | solution.py:324
  2.0 14.7 %all_to_all.30.rows_ref = bf16[4,48,256]{2,1,0:T(8,128)(2,1)S(1)} all-to-all(bf16[4,48,256]{2,1,0:T(8,128)(2,1)} %get-tuple-element.19), channel_id=1, replica_groups=mesh['y_lo'=2,'x'=4,'y_hi'=4,'z'=8,'core'=2] {'y_hi'}, dimensions={0} | all-to-all | bytes 196608 | tf_op jit(solution)/shard_map/all_to_all | solution.py:334
  16.7 0.9 regroup.1
  17.6 13.0 %all-to-all-start.1 = ((bf16[16,96,256]{2,1,0:T(8,128)(2,1)}), bf16[16,96,256]{2,1,0:T(8,128)(2,1)S(1)}, u32[]{:S(2)}, u32[]{:S(2)}) async-start(bf16[16,96,256]{2,1,0:T(8,128)(2,1)} %regroup.1), calls=%async_computation.1 | async-start | bytes 1572864 | tf_op jit(solution)/shard_map/all_to_all | solution.py:343
  30.6 2.0 %collective-permute-start = (bf16[392,256]{1,0:T(8,128)(2,1)S(1)}, bf16[392,256]{1,0:T(8,128)(2,1)S(1)}, u32[]{:S(2)}, u32[]{:S(2)}) collective-permute-start(bf16[392,256]{1,0:T(8,128)(2,1)S(1)} %copy-done.2), channel_id=1, source_target_pairs={{0,1},{1,0},{2,3},{3,2},{4,5},{5,4},{6,7},{7,6},{8,9},{9,8},{10,11... | collective-permute-start | bytes 602120 | tf_op jit(solution)/shard_map/ppermute | solution.py:344
  32.6 1.3 collective-permute-done.arrived_ref
  33.9 0.1 arrange.1
  34.0 2.0 %collective-permute-start.5 = (bf16[272,256]{1,0:T(8,128)(2,1)S(1)}, bf16[272,256]{1,0:T(8,128)(2,1)S(1)}, u32[]{:S(2)}, u32[]{:S(2)}) collective-permute-start(bf16[272,256]{1,0:T(8,128)(2,1)S(1)} %get-tuple-element.18.p0_ref), channel_id=1, source_target_pairs={{0,16},{16,32},{32,48},{48,0},{1,17},{17,33},{33,49},{49,1},{2,18}... | collective-permute-start | bytes 417800 | tf_op jit(solution)/shard_map/ppermute | solution.py:355
  36.0 3.8 %collective-permute-start.6 = (bf16[272,256]{1,0:T(8,128)(2,1)S(1)}, bf16[272,256]{1,0:T(8,128)(2,1)S(1)}, u32[]{:S(2)}, u32[]{:S(2)}) collective-permute-start(bf16[272,256]{1,0:T(8,128)(2,1)S(1)} %get-tuple-element.18.p0_ref), channel_id=1, source_target_pairs={{0,32},{16,48},{32,0},{48,16},{1,33},{17,49},{33,1},{49,17},{2,34}... | collective-permute-start | bytes 417800 | tf_op jit(solution)/shard_map/ppermute | solution.py:355
  39.9 3.6 %collective-permute-start.7 = (bf16[272,256]{1,0:T(8,128)(2,1)S(1)}, bf16[272,256]{1,0:T(8,128)(2,1)S(1)}, u32[]{:S(2)}, u32[]{:S(2)}) collective-permute-start(bf16[272,256]{1,0:T(8,128)(2,1)S(1)} %get-tuple-element.18.p0_ref), channel_id=1, source_target_pairs={{0,48},{16,0},{32,16},{48,32},{1,49},{17,1},{33,17},{49,33},{2,50}... | collective-permute-start | bytes 417800 | tf_op jit(solution)/shard_map/ppermute | solution.py:355
  43.5 1.9 %collective-permute-done.5.p1_ref = bf16[272,256]{1,0:T(8,128)(2,1)S(1)} collective-permute-done((bf16[272,256]{1,0:T(8,128)(2,1)S(1)}, bf16[272,256]{1,0:T(8,128)(2,1)S(1)}, u32[]{:S(2)}, u32[]{:S(2)}) %collective-permute-start.5) | collective-permute-done | bytes 139296 | tf_op jit(solution)/shard_map/ppermute | solution.py:355
  45.4 4.8 %collective-permute-done.6.p2_ref = bf16[272,256]{1,0:T(8,128)(2,1)S(1)} collective-permute-done((bf16[272,256]{1,0:T(8,128)(2,1)S(1)}, bf16[272,256]{1,0:T(8,128)(2,1)S(1)}, u32[]{:S(2)}, u32[]{:S(2)}) %collective-permute-start.6) | collective-permute-done | bytes 139296 | tf_op jit(solution)/shard_map/ppermute | solution.py:355
  50.2 6.3 %collective-permute-done.7.p3_ref = bf16[272,256]{1,0:T(8,128)(2,1)S(1)} collective-permute-done((bf16[272,256]{1,0:T(8,128)(2,1)S(1)}, bf16[272,256]{1,0:T(8,128)(2,1)S(1)}, u32[]{:S(2)}, u32[]{:S(2)}) %collective-permute-start.7) | collective-permute-done | bytes 139296 | tf_op jit(solution)/shard_map/ppermute | solution.py:355
  56.5 1.3 grad.1
  57.8 15.7 %all_to_all.31.parts_ref = bf16[8,96,128]{2,1,0:T(8,128)(2,1)S(1)} all-to-all(bf16[8,96,128]{2,1,0:T(8,128)(2,1)S(1)} %get-tuple-element.22), channel_id=1, replica_groups=mesh['y_lo'=2,'x'=4,'y_hi'=4,'z'=8,'core'=2] {'z'}, dimensions={0} | all-to-all | bytes 393216 | tf_op jit(solution)/shard_map/all_to_all | solution.py:367
  73.5 11.2 %all_to_all.32.piece_ref = bf16[8,96,128]{2,1,0:T(8,128)(2,1)S(1)} all-to-all(bf16[8,96,128]{2,1,0:T(8,128)(2,1)S(1)} %sum.1), channel_id=1, replica_groups=mesh['y_lo'=2,'x'=4,'y_hi'=4,'z'=8,'core'=2] {'z'}, dimensions={0} | all-to-all | bytes 393216 | tf_op jit(solution)/shard_map/all_to_all | solution.py:377
  84.8 1.0 widen.1
  85.8 3.5 %all-to-all-start.4 = ((bf16[4,8,96,128]{3,2,1,0:T(8,128)(2,1)}), bf16[4,8,96,128]{3,2,1,0:T(8,128)(2,1)S(1)}, u32[]{:S(2)}, u32[]{:S(2)}) async-start(bf16[4,8,96,128]{3,2,1,0:T(8,128)(2,1)} %widen.1), calls=%async_computation.4 | async-start | bytes 1572864 | tf_op jit(solution)/shard_map/all_to_all | solution.py:387
  89.3 2.0 %collective-permute-start.1 = (bf16[2,256,256]{2,1,0:T(8,128)(2,1)S(1)}, bf16[2,256,256]{2,1,0:T(8,128)(2,1)S(1)}, u32[]{:S(2)}, u32[]{:S(2)}) collective-permute-start(bf16[2,256,256]{2,1,0:T(8,128)(2,1)S(1)} %get-tuple-element.17), channel_id=1, source_target_pairs={{0,2},{2,4},{4,6},{6,8},{8,10},{10,12},{12,14},{14,16},{16,18},{18... | collective-permute-start | bytes 786440 | tf_op jit(solution)/shard_map/ppermute | solution.py:357
  91.3 16.0 %collective-permute-done.1 = bf16[2,256,256]{2,1,0:T(8,128)(2,1)S(1)} collective-permute-done((bf16[2,256,256]{2,1,0:T(8,128)(2,1)S(1)}, bf16[2,256,256]{2,1,0:T(8,128)(2,1)S(1)}, u32[]{:S(2)}, u32[]{:S(2)}) %collective-permute-start.1) | collective-permute-done | bytes 262176 | tf_op jit(solution)/shard_map/ppermute | solution.py:357
  107.3 1.9 %collective-permute-start.2 = (bf16[2,256,256]{2,1,0:T(8,128)(2,1)S(1)}, bf16[2,256,256]{2,1,0:T(8,128)(2,1)S(1)}, u32[]{:S(2)}, u32[]{:S(2)}) collective-permute-start(bf16[2,256,256]{2,1,0:T(8,128)(2,1)S(1)} %collective-permute-done.1), channel_id=1, source_target_pairs={{0,2},{2,4},{4,6},{6,8},{8,10},{10,12},{12,14},{14,16},{16,18},{18... | collective-permute-start | bytes 786440 | tf_op jit(solution)/shard_map/ppermute | solution.py:368
  109.2 14.6 %collective-permute-done.2 = bf16[2,256,256]{2,1,0:T(8,128)(2,1)S(1)} collective-permute-done((bf16[2,256,256]{2,1,0:T(8,128)(2,1)S(1)}, bf16[2,256,256]{2,1,0:T(8,128)(2,1)S(1)}, u32[]{:S(2)}, u32[]{:S(2)}) %collective-permute-start.2) | collective-permute-done | bytes 262176 | tf_op jit(solution)/shard_map/ppermute | solution.py:368
  123.8 1.9 %collective-permute-start.3 = (bf16[2,256,256]{2,1,0:T(8,128)(2,1)S(1)}, bf16[2,256,256]{2,1,0:T(8,128)(2,1)S(1)}, u32[]{:S(2)}, u32[]{:S(2)}) collective-permute-start(bf16[2,256,256]{2,1,0:T(8,128)(2,1)S(1)} %collective-permute-done.2), channel_id=1, source_target_pairs={{0,2},{2,4},{4,6},{6,8},{8,10},{10,12},{12,14},{14,16},{16,18},{18... | collective-permute-start | bytes 786440 | tf_op jit(solution)/shard_map/ppermute | solution.py:378
  125.7 0.6 copy-done.3
  126.4 0.6 dynamic_slice.3.step_ref
  127.0 8.2 %collective-permute-done.3._ = bf16[2,256,256]{2,1,0:T(8,128)(2,1)S(1)} collective-permute-done((bf16[2,256,256]{2,1,0:T(8,128)(2,1)S(1)}, bf16[2,256,256]{2,1,0:T(8,128)(2,1)S(1)}, u32[]{:S(2)}, u32[]{:S(2)}) %collective-permute-start.3) | collective-permute-done | bytes 262176 | tf_op jit(solution)/shard_map/ppermute | solution.py:378
  135.2 1.9 %collective-permute-start.4 = (bf16[2,256,256]{2,1,0:T(8,128)(2,1)S(1)}, bf16[2,256,256]{2,1,0:T(8,128)(2,1)S(1)}, u32[]{:S(2)}, u32[]{:S(2)}) collective-permute-start(bf16[2,256,256]{2,1,0:T(8,128)(2,1)S(1)} %collective-permute-done.3._), channel_id=1, source_target_pairs={{0,2},{2,4},{4,6},{6,8},{8,10},{10,12},{12,14},{14,16},{16,18},{18... | collective-permute-start | bytes 786440 | tf_op jit(solution)/shard_map/ppermute | solution.py:402
  137.2 7.4 %newton.1.fast_ref = f32[128,256]{1,0:T(8,128)S(1)} custom-call(f32[1]{0:T(128)} %dynamic_slice.3.step_ref, bf16[4,8,96,128]{3,2,1,0:T(8,128)(2,1)S(1)} %all-to-all-done.4.total_ref, bf16[4,512,128]{2,1,0:T(8,128)(2,1)S(1)} %get-tuple-element.20.slices_ref, bf16[512,256]{1,0:T(8,128)(2,1)S(1)} %get-tuple-element.21.down_ref, ...), custom_call_target="tpu_custom_call" | custom-call | flops 8000000000 | bytes 4000000 | tf_op jit(solution)/shard_map/newton/pallas_call | solution.py:390
  144.6 5.2 %collective-permute-done.4 = bf16[2,256,256]{2,1,0:T(8,128)(2,1)S(1)} collective-permute-done((bf16[2,256,256]{2,1,0:T(8,128)(2,1)S(1)}, bf16[2,256,256]{2,1,0:T(8,128)(2,1)S(1)}, u32[]{:S(2)}, u32[]{:S(2)}) %collective-permute-start.4) | collective-permute-done | bytes 262176 | tf_op jit(solution)/shard_map/ppermute | solution.py:402
  149.8 1.3 window.1
  151.1 19.7 %all_to_all.33.parts_ref = bf16[16,2,8,256]{3,2,1,0:T(8,128)(2,1)S(1)} all-to-all(bf16[16,2,8,256]{3,2,1,0:T(8,128)(2,1)S(1)} %window.1), channel_id=1, replica_groups=mesh['y_lo'=2,'x'=4,'y_hi'=4,'z'=8,'core'=2] {'core','y_lo','x'}, dimensions={0} | all-to-all | bytes 262144 | tf_op jit(solution)/shard_map/all_to_all | solution.py:412
  170.8 0.8 norm.1
  (10 shorter events, 0.1 us)
Async XLA Ops:
  17.6 13.0 %copy-start.2 = (bf16[392,256]{1,0:T(8,128)(2,1)S(1)}, bf16[392,256]{1,0:T(8,128)(2,1)}, u32[]{:S(2)}) copy-start(bf16[392,256]{1,0:T(8,128)(2,1)} %get-tuple-element.15) | copy-start | bytes 602116
  17.6 16.3 %copy-start = (bf16[392,256]{1,0:T(8,128)(2,1)S(1)}, bf16[392,256]{1,0:T(8,128)(2,1)}, u32[]{:S(2)}) copy-start(bf16[392,256]{1,0:T(8,128)(2,1)} %get-tuple-element.14.mine_ref) | copy-start | bytes 602116
  17.6 38.9 %all-to-all-start.1 = ((bf16[16,96,256]{2,1,0:T(8,128)(2,1)}), bf16[16,96,256]{2,1,0:T(8,128)(2,1)S(1)}, u32[]{:S(2)}, u32[]{:S(2)}) async-start(bf16[16,96,256]{2,1,0:T(8,128)(2,1)} %regroup.1), calls=%async_computation.1 | async-start | bytes 1572864 | tf_op jit(solution)/shard_map/all_to_all | solution.py:343
  30.6 3.3 %collective-permute-start = (bf16[392,256]{1,0:T(8,128)(2,1)S(1)}, bf16[392,256]{1,0:T(8,128)(2,1)S(1)}, u32[]{:S(2)}, u32[]{:S(2)}) collective-permute-start(bf16[392,256]{1,0:T(8,128)(2,1)S(1)} %copy-done.2), channel_id=1, source_target_pairs={{0,1},{1,0},{2,3},{3,2},{4,5},{5,4},{6,7},{7,6},{8,9},{9,8},{10,11... | collective-permute-start | bytes 602120 | tf_op jit(solution)/shard_map/ppermute | solution.py:344
  34.0 11.4 %collective-permute-start.5 = (bf16[272,256]{1,0:T(8,128)(2,1)S(1)}, bf16[272,256]{1,0:T(8,128)(2,1)S(1)}, u32[]{:S(2)}, u32[]{:S(2)}) collective-permute-start(bf16[272,256]{1,0:T(8,128)(2,1)S(1)} %get-tuple-element.18.p0_ref), channel_id=1, source_target_pairs={{0,16},{16,32},{32,48},{48,0},{1,17},{17,33},{33,49},{49,1},{2,18}... | collective-permute-start | bytes 417800 | tf_op jit(solution)/shard_map/ppermute | solution.py:355
  36.0 14.2 %collective-permute-start.6 = (bf16[272,256]{1,0:T(8,128)(2,1)S(1)}, bf16[272,256]{1,0:T(8,128)(2,1)S(1)}, u32[]{:S(2)}, u32[]{:S(2)}) collective-permute-start(bf16[272,256]{1,0:T(8,128)(2,1)S(1)} %get-tuple-element.18.p0_ref), channel_id=1, source_target_pairs={{0,32},{16,48},{32,0},{48,16},{1,33},{17,49},{33,1},{49,17},{2,34}... | collective-permute-start | bytes 417800 | tf_op jit(solution)/shard_map/ppermute | solution.py:355
  39.9 16.7 %collective-permute-start.7 = (bf16[272,256]{1,0:T(8,128)(2,1)S(1)}, bf16[272,256]{1,0:T(8,128)(2,1)S(1)}, u32[]{:S(2)}, u32[]{:S(2)}) collective-permute-start(bf16[272,256]{1,0:T(8,128)(2,1)S(1)} %get-tuple-element.18.p0_ref), channel_id=1, source_target_pairs={{0,48},{16,0},{32,16},{48,32},{1,49},{17,1},{33,17},{49,33},{2,50}... | collective-permute-start | bytes 417800 | tf_op jit(solution)/shard_map/ppermute | solution.py:355
  85.8 51.4 %all-to-all-start.4 = ((bf16[4,8,96,128]{3,2,1,0:T(8,128)(2,1)}), bf16[4,8,96,128]{3,2,1,0:T(8,128)(2,1)S(1)}, u32[]{:S(2)}, u32[]{:S(2)}) async-start(bf16[4,8,96,128]{3,2,1,0:T(8,128)(2,1)} %widen.1), calls=%async_computation.4 | async-start | bytes 1572864 | tf_op jit(solution)/shard_map/all_to_all | solution.py:387
  89.3 18.0 %collective-permute-start.1 = (bf16[2,256,256]{2,1,0:T(8,128)(2,1)S(1)}, bf16[2,256,256]{2,1,0:T(8,128)(2,1)S(1)}, u32[]{:S(2)}, u32[]{:S(2)}) collective-permute-start(bf16[2,256,256]{2,1,0:T(8,128)(2,1)S(1)} %get-tuple-element.17), channel_id=1, source_target_pairs={{0,2},{2,4},{4,6},{6,8},{8,10},{10,12},{12,14},{14,16},{16,18},{18... | collective-permute-start | bytes 786440 | tf_op jit(solution)/shard_map/ppermute | solution.py:357
  107.3 16.5 %collective-permute-start.2 = (bf16[2,256,256]{2,1,0:T(8,128)(2,1)S(1)}, bf16[2,256,256]{2,1,0:T(8,128)(2,1)S(1)}, u32[]{:S(2)}, u32[]{:S(2)}) collective-permute-start(bf16[2,256,256]{2,1,0:T(8,128)(2,1)S(1)} %collective-permute-done.1), channel_id=1, source_target_pairs={{0,2},{2,4},{4,6},{6,8},{8,10},{10,12},{12,14},{14,16},{16,18},{18... | collective-permute-start | bytes 786440 | tf_op jit(solution)/shard_map/ppermute | solution.py:368
  123.8 11.4 %collective-permute-start.3 = (bf16[2,256,256]{2,1,0:T(8,128)(2,1)S(1)}, bf16[2,256,256]{2,1,0:T(8,128)(2,1)S(1)}, u32[]{:S(2)}, u32[]{:S(2)}) collective-permute-start(bf16[2,256,256]{2,1,0:T(8,128)(2,1)S(1)} %collective-permute-done.2), channel_id=1, source_target_pairs={{0,2},{2,4},{4,6},{6,8},{8,10},{10,12},{12,14},{14,16},{16,18},{18... | collective-permute-start | bytes 786440 | tf_op jit(solution)/shard_map/ppermute | solution.py:378
  125.7 0.7 copy-start.3
  135.2 14.6 %collective-permute-start.4 = (bf16[2,256,256]{2,1,0:T(8,128)(2,1)S(1)}, bf16[2,256,256]{2,1,0:T(8,128)(2,1)S(1)}, u32[]{:S(2)}, u32[]{:S(2)}) collective-permute-start(bf16[2,256,256]{2,1,0:T(8,128)(2,1)S(1)} %collective-permute-done.3._), channel_id=1, source_target_pairs={{0,2},{2,4},{4,6},{6,8},{8,10},{10,12},{12,14},{14,16},{16,18},{18... | collective-permute-start | bytes 786440 | tf_op jit(solution)/shard_map/ppermute | solution.py:402
  151.1 19.7 %copy-start.1 = (f32[4096]{0:T(1024)S(1)}, f32[4096]{0:T(1024)}, u32[]{:S(2)}) copy-start(f32[4096]{0:T(1024)} %param.17) | copy-start | bytes 49156
where the time goes:
time: 174 us; the launch traced here: 172 us
  blocking collectives  61.3 us (35%)
  waiting for transfers between devices  58.3 us (34%)
  starting transfers between devices  35.8 us (21%)
  Pallas kernels  14.8 us (9%)
    ppermute x3, waiting for transfers between devices, body(): chunks.append(lax.ppermute(chunks[-1], RING, ring))  28 us
    all_to_all x1, blocking collectives, body(): gathered = lax.all_to_all(combined, ('core', 'y_lo', 'x'), 0, 0, tiled=True)  19.7 us
    ppermute x1, waiting for transfers between devices, body(): chunks = [lax.ppermute(context, RING, ring)]  16 us
    all_to_all x1, blocking collectives, body(): parts = lax.all_to_all(grad, 'z', 0, 0, tiled=True)  15.7 us
    all_to_all x1, blocking collectives, body(): dealt = lax.all_to_all(dealt, 'y_hi', 0, 0, tiled=True)  14.7 us
    ppermute x3, waiting for transfers between devices, body(): lax.ppermute(pool, 'y_hi', [(i, (i + distance) % 4) for i in range(4)])  13 us
    all_to_all x1, starting transfers between devices, body(): dealt = lax.all_to_all(dealt, ('z', 'core'), 0, 0, tiled=True)  13 us
    all_to_all x1, blocking collectives, body(): total = lax.all_to_all(total, 'z', 0, 0, tiled=True)  11.2 us
  transfers between devices with their start and end apart: 10, of which 8 were waited for; matrix products, arithmetic and copies ran while one was open for 0% of the time, Pallas kernels for 4%

commit v1 on v0

--- a/solution.py
+++ b/solution.py
@@ -189,7 +189,7 @@
 
 
 def attention_kernel(
-    chip_ref, own_ref, c1_ref, c2_ref, c3_ref, c4_ref, slices_ref, down_ref, fast_ref, out_ref
+    chip_ref, own_ref, c1_ref, c2_ref, c3_ref, c4_ref, slices_ref, down_ref, out_ref
 ):
     chip = chip_ref[0]
     row = lax.broadcasted_iota(jnp.int32, (TOK, TOK), 0)
@@ -236,9 +236,7 @@
             result = part if result is None else result + part
         if block == 0:
             result = result + fast_forward(query, *whole_weights(slices_ref), down_ref[...])
-        else:
-            result = result + fast_ref[...]
-        out_ref[:, block] = result.reshape(16, 8, DH).astype(BF)
+        out_ref[block] = result
 
 
 def coarse_step(iterates):
@@ -266,7 +264,7 @@
 
 
 def newton_kernel(
-    step_ref, total_ref, slices_ref, down_ref, own_ref, _, fast_ref, iterate_ref
+    step_ref, total_ref, slices_ref, down_ref, own_ref, base_ref, out_ref, iterate_ref
 ):
     for index in range(3):
         rows = slice(index * 32, index * 32 + 32)
@@ -287,7 +285,9 @@
     up_fast = (up_fast.astype(F32) + step * iterate_ref[1]).astype(BF)
     down_fast = (down_ref[...].astype(F32) + step * iterate_ref[2].T).astype(BF)
     query = jnp.concatenate([own_ref[0, 64:128, :], own_ref[1, 64:128, :]], 0)
-    fast_ref[...] = fast_forward(query, gate_fast, up_fast, down_fast)
+    fast = fast_forward(query, gate_fast, up_fast, down_fast)
+    out_ref[:, 0] = base_ref[0].reshape(16, 8, DH).astype(BF)
+    out_ref[:, 1] = (fast + base_ref[1]).reshape(16, 8, DH).astype(BF)
 
 
 def norm_kernel(parts_ref, gain_ref, out_ref):
@@ -386,29 +386,26 @@
     )(total)
     total = lax.all_to_all(total, "y_hi", 0, 0, tiled=True)
 
-    step = lax.dynamic_slice_in_dim(step_size, core, 1, 0)
-    fast = pl.pallas_call(
-        newton_kernel,
-        out_shape=shape_of((TOK, DH), F32),
-        in_specs=[SMEM] + [VMEM] * 4 + [ANY],
-        out_specs=VMEM,
-        scratch_shapes=[pltpu.VMEM((3, DH, DF), F32)],
-        compiler_params=PARAMS,
-        cost_estimate=pl.CostEstimate(
-            flops=8_000_000_000, transcendentals=100_000, bytes_accessed=4_000_000
-        ),
-        name="newton",
-    )(step, total, slices, down_fast, own, chunks[2])
     chunks.append(lax.ppermute(chunks[-1], RING, ring))
     chunks = [chunk.reshape(2, 4, 64, DH) for chunk in chunks]
+    base = pl.pallas_call(
+        attention_kernel,
+        out_shape=shape_of((2, TOK, DH), F32),
+        in_specs=[SMEM] + [VMEM] * 7,
+        out_specs=VMEM,
+        compiler_params=PARAMS,
+        name="window",
+    )(chip, own, *chunks, slices, down_fast)
+    step = lax.dynamic_slice_in_dim(step_size, core, 1, 0)
     combined = pl.pallas_call(
-        attention_kernel,
+        newton_kernel,
         out_shape=shape_of((16, 2, 8, DH)),
-        in_specs=[SMEM] + [VMEM] * 8,
-        out_specs=VMEM,
-        compiler_params=PARAMS,
-        name="window",
-    )(chip, own, *chunks, slices, down_fast, fast)
+        in_specs=[SMEM] + [VMEM] * 5,
+        out_specs=VMEM,
+        scratch_shapes=[pltpu.VMEM((3, DH, DF), F32)],
+        compiler_params=PARAMS,
+        name="newton",
+    )(step, total, slices, down_fast, own, base)
     gathered = lax.all_to_all(combined, ("core", "y_lo", "x"), 0, 0, tiled=True)
     return pl.pallas_call(
         norm_kernel,

time: 174 us -> 182 us (1.046)
  waiting for transfers between devices: 58.3 us -> 65.8 us
    ppermute x3, waiting for transfers between devices: 28 us -> 35.5 us  [body(): chunks.append(lax.ppermute(chunks[-1], RING, ring))]
  transfers between devices with their start and end apart: 10 -> 10, of which waited for: 8 -> 8; matrix products, arithmetic and copies ran while one was open for 0% -> 0% of each run, Pallas kernels for 4% -> 1%
where the time goes in v1:
time: 182 us; the launch traced here: 179 us
  waiting for transfers between devices  65.8 us (36%)
  blocking collectives  61.3 us (34%)
  starting transfers between devices  35.8 us (20%)
  Pallas kernels  14.8 us (8%)
    ppermute x3, waiting for transfers between devices, body(): chunks.append(lax.ppermute(chunks[-1], RING, ring))  35.5 us
    all_to_all x1, blocking collectives, body(): gathered = lax.all_to_all(combined, ('core', 'y_lo', 'x'), 0, 0, tiled=True)  19.7 us
    ppermute x1, waiting for transfers between devices, body(): chunks = [lax.ppermute(context, RING, ring)]  16 us
    all_to_all x1, blocking collectives, body(): parts = lax.all_to_all(grad, 'z', 0, 0, tiled=True)  15.7 us
    all_to_all x1, blocking collectives, body(): dealt = lax.all_to_all(dealt, 'y_hi', 0, 0, tiled=True)  14.7 us
    ppermute x3, waiting for transfers between devices, body(): lax.ppermute(pool, 'y_hi', [(i, (i + distance) % 4) for i in range(4)])  13 us
    all_to_all x1, starting transfers between devices, body(): dealt = lax.all_to_all(dealt, ('z', 'core'), 0, 0, tiled=True)  13 us
    all_to_all x1, blocking collectives, body(): total = lax.all_to_all(total, 'z', 0, 0, tiled=True)  11.2 us
  transfers between devices with their start and end apart: 10, of which 8 were waited for; matrix products, arithmetic and copies ran while one was open for 0% of the time, Pallas kernels for 1%

profile of v1, /device:TPU:1, one launch (start us, length us, event | category | flops | bytes accessed | tf_op | source)
XLA Modules:
  0.0 179.1 jit_solution(7450216568706054696)
XLA Ops:
  0.0 2.0 %pack.1 = (bf16[392,256]{1,0:T(8,128)(2,1)}, bf16[392,256]{1,0:T(8,128)(2,1)}, bf16[4,48,256]{2,1,0:T(8,128)(2,1)}) custom-call(s32[1]{0:T(128)} %bitcast.1.core_ref, bf16[2,64,512]{2,1,0:T(8,128)(2,1)} %q_in.1, bf16[2,64,512]{2,1,0:T(8,128)(2,1)} %k_in.1, bf16[2,64,512]{2,1,0:T(8,128)(2,1)} %v_in.1, f32[1,2,64]{2,1,0:T(2,128)} %rate_in.1, ...), custom_call_target="tpu_custom_call" | custom-call | tf_op jit(solution)/shard_map/pack/pallas_call | solution.py:324
  2.0 14.7 %all_to_all.30.rows_ref = bf16[4,48,256]{2,1,0:T(8,128)(2,1)S(1)} all-to-all(bf16[4,48,256]{2,1,0:T(8,128)(2,1)} %get-tuple-element.17), channel_id=1, replica_groups=mesh['y_lo'=2,'x'=4,'y_hi'=4,'z'=8,'core'=2] {'y_hi'}, dimensions={0} | all-to-all | bytes 196608 | tf_op jit(solution)/shard_map/all_to_all | solution.py:334
  16.7 0.9 regroup.1
  17.6 13.0 %all-to-all-start.1 = ((bf16[16,96,256]{2,1,0:T(8,128)(2,1)}), bf16[16,96,256]{2,1,0:T(8,128)(2,1)S(1)}, u32[]{:S(2)}, u32[]{:S(2)}) async-start(bf16[16,96,256]{2,1,0:T(8,128)(2,1)} %regroup.1), calls=%async_computation.1 | async-start | bytes 1572864 | tf_op jit(solution)/shard_map/all_to_all | solution.py:343
  30.6 2.0 %collective-permute-start = (bf16[392,256]{1,0:T(8,128)(2,1)S(1)}, bf16[392,256]{1,0:T(8,128)(2,1)S(1)}, u32[]{:S(2)}, u32[]{:S(2)}) collective-permute-start(bf16[392,256]{1,0:T(8,128)(2,1)S(1)} %copy-done.2), channel_id=1, source_target_pairs={{0,1},{1,0},{2,3},{3,2},{4,5},{5,4},{6,7},{7,6},{8,9},{9,8},{10,11... | collective-permute-start | bytes 602120 | tf_op jit(solution)/shard_map/ppermute | solution.py:344
  32.6 1.3 collective-permute-done.arrived_ref
  33.9 0.1 arrange.1
  34.0 2.0 %collective-permute-start.1 = (bf16[272,256]{1,0:T(8,128)(2,1)S(1)}, bf16[272,256]{1,0:T(8,128)(2,1)S(1)}, u32[]{:S(2)}, u32[]{:S(2)}) collective-permute-start(bf16[272,256]{1,0:T(8,128)(2,1)S(1)} %get-tuple-element.16.p0_ref), channel_id=1, source_target_pairs={{0,16},{16,32},{32,48},{48,0},{1,17},{17,33},{33,49},{49,1},{2,18}... | collective-permute-start | bytes 417800 | tf_op jit(solution)/shard_map/ppermute | solution.py:355
  36.0 3.8 %collective-permute-start.2 = (bf16[272,256]{1,0:T(8,128)(2,1)S(1)}, bf16[272,256]{1,0:T(8,128)(2,1)S(1)}, u32[]{:S(2)}, u32[]{:S(2)}) collective-permute-start(bf16[272,256]{1,0:T(8,128)(2,1)S(1)} %get-tuple-element.16.p0_ref), channel_id=1, source_target_pairs={{0,32},{16,48},{32,0},{48,16},{1,33},{17,49},{33,1},{49,17},{2,34}... | collective-permute-start | bytes 417800 | tf_op jit(solution)/shard_map/ppermute | solution.py:355
  39.9 3.6 %collective-permute-start.3 = (bf16[272,256]{1,0:T(8,128)(2,1)S(1)}, bf16[272,256]{1,0:T(8,128)(2,1)S(1)}, u32[]{:S(2)}, u32[]{:S(2)}) collective-permute-start(bf16[272,256]{1,0:T(8,128)(2,1)S(1)} %get-tuple-element.16.p0_ref), channel_id=1, source_target_pairs={{0,48},{16,0},{32,16},{48,32},{1,49},{17,1},{33,17},{49,33},{2,50}... | collective-permute-start | bytes 417800 | tf_op jit(solution)/shard_map/ppermute | solution.py:355
  43.5 1.9 %collective-permute-done.1.p1_ref = bf16[272,256]{1,0:T(8,128)(2,1)S(1)} collective-permute-done((bf16[272,256]{1,0:T(8,128)(2,1)S(1)}, bf16[272,256]{1,0:T(8,128)(2,1)S(1)}, u32[]{:S(2)}, u32[]{:S(2)}) %collective-permute-start.1) | collective-permute-done | bytes 139296 | tf_op jit(solution)/shard_map/ppermute | solution.py:355
  45.4 4.8 %collective-permute-done.2.p2_ref = bf16[272,256]{1,0:T(8,128)(2,1)S(1)} collective-permute-done((bf16[272,256]{1,0:T(8,128)(2,1)S(1)}, bf16[272,256]{1,0:T(8,128)(2,1)S(1)}, u32[]{:S(2)}, u32[]{:S(2)}) %collective-permute-start.2) | collective-permute-done | bytes 139296 | tf_op jit(solution)/shard_map/ppermute | solution.py:355
  50.2 6.3 %collective-permute-done.3.p3_ref = bf16[272,256]{1,0:T(8,128)(2,1)S(1)} collective-permute-done((bf16[272,256]{1,0:T(8,128)(2,1)S(1)}, bf16[272,256]{1,0:T(8,128)(2,1)S(1)}, u32[]{:S(2)}, u32[]{:S(2)}) %collective-permute-start.3) | collective-permute-done | bytes 139296 | tf_op jit(solution)/shard_map/ppermute | solution.py:355
  56.5 1.3 grad.1
  57.8 15.7 %all_to_all.31.parts_ref = bf16[8,96,128]{2,1,0:T(8,128)(2,1)S(1)} all-to-all(bf16[8,96,128]{2,1,0:T(8,128)(2,1)S(1)} %get-tuple-element.18), channel_id=1, replica_groups=mesh['y_lo'=2,'x'=4,'y_hi'=4,'z'=8,'core'=2] {'z'}, dimensions={0} | all-to-all | bytes 393216 | tf_op jit(solution)/shard_map/all_to_all | solution.py:367
  73.5 11.2 %all_to_all.32.piece_ref = bf16[8,96,128]{2,1,0:T(8,128)(2,1)S(1)} all-to-all(bf16[8,96,128]{2,1,0:T(8,128)(2,1)S(1)} %sum.1), channel_id=1, replica_groups=mesh['y_lo'=2,'x'=4,'y_hi'=4,'z'=8,'core'=2] {'z'}, dimensions={0} | all-to-all | bytes 393216 | tf_op jit(solution)/shard_map/all_to_all | solution.py:377
  84.8 1.0 widen.1
  85.8 3.5 %all-to-all-start.4 = ((bf16[4,8,96,128]{3,2,1,0:T(8,128)(2,1)}), bf16[4,8,96,128]{3,2,1,0:T(8,128)(2,1)S(1)}, u32[]{:S(2)}, u32[]{:S(2)}) async-start(bf16[4,8,96,128]{3,2,1,0:T(8,128)(2,1)} %widen.1), calls=%async_computation.4 | async-start | bytes 1572864 | tf_op jit(solution)/shard_map/all_to_all | solution.py:387
  89.3 2.0 %collective-permute-start.4 = (bf16[2,256,256]{2,1,0:T(8,128)(2,1)S(1)}, bf16[2,256,256]{2,1,0:T(8,128)(2,1)S(1)}, u32[]{:S(2)}, u32[]{:S(2)}) collective-permute-start(bf16[2,256,256]{2,1,0:T(8,128)(2,1)S(1)} %get-tuple-element.22), channel_id=1, source_target_pairs={{0,2},{2,4},{4,6},{6,8},{8,10},{10,12},{12,14},{14,16},{16,18},{18... | collective-permute-start | bytes 786440 | tf_op jit(solution)/shard_map/ppermute | solution.py:357
  91.3 16.0 %collective-permute-done.4 = bf16[2,256,256]{2,1,0:T(8,128)(2,1)S(1)} collective-permute-done((bf16[2,256,256]{2,1,0:T(8,128)(2,1)S(1)}, bf16[2,256,256]{2,1,0:T(8,128)(2,1)S(1)}, u32[]{:S(2)}, u32[]{:S(2)}) %collective-permute-start.4) | collective-permute-done | bytes 262176 | tf_op jit(solution)/shard_map/ppermute | solution.py:357
  107.3 1.9 %collective-permute-start.5 = (bf16[2,256,256]{2,1,0:T(8,128)(2,1)S(1)}, bf16[2,256,256]{2,1,0:T(8,128)(2,1)S(1)}, u32[]{:S(2)}, u32[]{:S(2)}) collective-permute-start(bf16[2,256,256]{2,1,0:T(8,128)(2,1)S(1)} %collective-permute-done.4), channel_id=1, source_target_pairs={{0,2},{2,4},{4,6},{6,8},{8,10},{10,12},{12,14},{14,16},{16,18},{18... | collective-permute-start | bytes 786440 | tf_op jit(solution)/shard_map/ppermute | solution.py:368
  109.2 14.6 %collective-permute-done.5 = bf16[2,256,256]{2,1,0:T(8,128)(2,1)S(1)} collective-permute-done((bf16[2,256,256]{2,1,0:T(8,128)(2,1)S(1)}, bf16[2,256,256]{2,1,0:T(8,128)(2,1)S(1)}, u32[]{:S(2)}, u32[]{:S(2)}) %collective-permute-start.5) | collective-permute-done | bytes 262176 | tf_op jit(solution)/shard_map/ppermute | solution.py:368
  123.8 1.9 %collective-permute-start.6 = (bf16[2,256,256]{2,1,0:T(8,128)(2,1)S(1)}, bf16[2,256,256]{2,1,0:T(8,128)(2,1)S(1)}, u32[]{:S(2)}, u32[]{:S(2)}) collective-permute-start(bf16[2,256,256]{2,1,0:T(8,128)(2,1)S(1)} %collective-permute-done.5), channel_id=1, source_target_pairs={{0,2},{2,4},{4,6},{6,8},{8,10},{10,12},{12,14},{14,16},{16,18},{18... | collective-permute-start | bytes 786440 | tf_op jit(solution)/shard_map/ppermute | solution.py:378
  125.7 9.5 %collective-permute-done.6 = bf16[2,256,256]{2,1,0:T(8,128)(2,1)S(1)} collective-permute-done((bf16[2,256,256]{2,1,0:T(8,128)(2,1)S(1)}, bf16[2,256,256]{2,1,0:T(8,128)(2,1)S(1)}, u32[]{:S(2)}, u32[]{:S(2)}) %collective-permute-start.6) | collective-permute-done | bytes 262176 | tf_op jit(solution)/shard_map/ppermute | solution.py:378
  135.2 1.9 %collective-permute-start.7 = (bf16[2,256,256]{2,1,0:T(8,128)(2,1)S(1)}, bf16[2,256,256]{2,1,0:T(8,128)(2,1)S(1)}, u32[]{:S(2)}, u32[]{:S(2)}) collective-permute-start(bf16[2,256,256]{2,1,0:T(8,128)(2,1)S(1)} %collective-permute-done.6), channel_id=1, source_target_pairs={{0,2},{2,4},{4,6},{6,8},{8,10},{10,12},{12,14},{14,16},{16,18},{18... | collective-permute-start | bytes 786440 | tf_op jit(solution)/shard_map/ppermute | solution.py:389
  137.2 0.6 copy-done.3
  137.8 0.6 dynamic_slice.3.step_ref
  138.4 11.4 %collective-permute-done.7 = bf16[2,256,256]{2,1,0:T(8,128)(2,1)S(1)} collective-permute-done((bf16[2,256,256]{2,1,0:T(8,128)(2,1)S(1)}, bf16[2,256,256]{2,1,0:T(8,128)(2,1)S(1)}, u32[]{:S(2)}, u32[]{:S(2)}) %collective-permute-start.7) | collective-permute-done | bytes 262176 | tf_op jit(solution)/shard_map/ppermute | solution.py:389
  149.8 1.3 window.1.base_ref
  151.1 7.5 %newton.1 = bf16[16,2,8,256]{3,2,1,0:T(8,128)(2,1)S(1)} custom-call(f32[1]{0:T(128)} %dynamic_slice.3.step_ref, bf16[4,8,96,128]{3,2,1,0:T(8,128)(2,1)S(1)} %all-to-all-done.4.total_ref, bf16[4,512,128]{2,1,0:T(8,128)(2,1)S(1)} %get-tuple-element.19.slices_ref, bf16[512,256]{1,0:T(8,128)(2,1)S(1)} %get-tuple-element.20.down_ref, ...), custom_call_target="tpu_custom_call" | custom-call | tf_op jit(solution)/shard_map/newton/pallas_call | solution.py:400
  158.6 19.7 %all_to_all.33.parts_ref = bf16[16,2,8,256]{3,2,1,0:T(8,128)(2,1)S(1)} all-to-all(bf16[16,2,8,256]{3,2,1,0:T(8,128)(2,1)S(1)} %newton.1), channel_id=1, replica_groups=mesh['y_lo'=2,'x'=4,'y_hi'=4,'z'=8,'core'=2] {'core','y_lo','x'}, dimensions={0} | all-to-all | bytes 262144 | tf_op jit(solution)/shard_map/all_to_all | solution.py:409
  178.3 0.8 norm.1
  (10 shorter events, 0.1 us)
Async XLA Ops:
  17.6 13.0 %copy-start.2 = (bf16[392,256]{1,0:T(8,128)(2,1)S(1)}, bf16[392,256]{1,0:T(8,128)(2,1)}, u32[]{:S(2)}) copy-start(bf16[392,256]{1,0:T(8,128)(2,1)} %get-tuple-element.15) | copy-start | bytes 602116
  17.6 16.3 %copy-start = (bf16[392,256]{1,0:T(8,128)(2,1)S(1)}, bf16[392,256]{1,0:T(8,128)(2,1)}, u32[]{:S(2)}) copy-start(bf16[392,256]{1,0:T(8,128)(2,1)} %get-tuple-element.14.mine_ref) | copy-start | bytes 602116
  17.6 38.9 %all-to-all-start.1 = ((bf16[16,96,256]{2,1,0:T(8,128)(2,1)}), bf16[16,96,256]{2,1,0:T(8,128)(2,1)S(1)}, u32[]{:S(2)}, u32[]{:S(2)}) async-start(bf16[16,96,256]{2,1,0:T(8,128)(2,1)} %regroup.1), calls=%async_computation.1 | async-start | bytes 1572864 | tf_op jit(solution)/shard_map/all_to_all | solution.py:343
  30.6 3.3 %collective-permute-start = (bf16[392,256]{1,0:T(8,128)(2,1)S(1)}, bf16[392,256]{1,0:T(8,128)(2,1)S(1)}, u32[]{:S(2)}, u32[]{:S(2)}) collective-permute-start(bf16[392,256]{1,0:T(8,128)(2,1)S(1)} %copy-done.2), channel_id=1, source_target_pairs={{0,1},{1,0},{2,3},{3,2},{4,5},{5,4},{6,7},{7,6},{8,9},{9,8},{10,11... | collective-permute-start | bytes 602120 | tf_op jit(solution)/shard_map/ppermute | solution.py:344
  34.0 11.4 %collective-permute-start.1 = (bf16[272,256]{1,0:T(8,128)(2,1)S(1)}, bf16[272,256]{1,0:T(8,128)(2,1)S(1)}, u32[]{:S(2)}, u32[]{:S(2)}) collective-permute-start(bf16[272,256]{1,0:T(8,128)(2,1)S(1)} %get-tuple-element.16.p0_ref), channel_id=1, source_target_pairs={{0,16},{16,32},{32,48},{48,0},{1,17},{17,33},{33,49},{49,1},{2,18}... | collective-permute-start | bytes 417800 | tf_op jit(solution)/shard_map/ppermute | solution.py:355
  36.0 14.2 %collective-permute-start.2 = (bf16[272,256]{1,0:T(8,128)(2,1)S(1)}, bf16[272,256]{1,0:T(8,128)(2,1)S(1)}, u32[]{:S(2)}, u32[]{:S(2)}) collective-permute-start(bf16[272,256]{1,0:T(8,128)(2,1)S(1)} %get-tuple-element.16.p0_ref), channel_id=1, source_target_pairs={{0,32},{16,48},{32,0},{48,16},{1,33},{17,49},{33,1},{49,17},{2,34}... | collective-permute-start | bytes 417800 | tf_op jit(solution)/shard_map/ppermute | solution.py:355
  39.9 16.7 %collective-permute-start.3 = (bf16[272,256]{1,0:T(8,128)(2,1)S(1)}, bf16[272,256]{1,0:T(8,128)(2,1)S(1)}, u32[]{:S(2)}, u32[]{:S(2)}) collective-permute-start(bf16[272,256]{1,0:T(8,128)(2,1)S(1)} %get-tuple-element.16.p0_ref), channel_id=1, source_target_pairs={{0,48},{16,0},{32,16},{48,32},{1,49},{17,1},{33,17},{49,33},{2,50}... | collective-permute-start | bytes 417800 | tf_op jit(solution)/shard_map/ppermute | solution.py:355
  85.8 65.4 %all-to-all-start.4 = ((bf16[4,8,96,128]{3,2,1,0:T(8,128)(2,1)}), bf16[4,8,96,128]{3,2,1,0:T(8,128)(2,1)S(1)}, u32[]{:S(2)}, u32[]{:S(2)}) async-start(bf16[4,8,96,128]{3,2,1,0:T(8,128)(2,1)} %widen.1), calls=%async_computation.4 | async-start | bytes 1572864 | tf_op jit(solution)/shard_map/all_to_all | solution.py:387
  89.3 18.0 %collective-permute-start.4 = (bf16[2,256,256]{2,1,0:T(8,128)(2,1)S(1)}, bf16[2,256,256]{2,1,0:T(8,128)(2,1)S(1)}, u32[]{:S(2)}, u32[]{:S(2)}) collective-permute-start(bf16[2,256,256]{2,1,0:T(8,128)(2,1)S(1)} %get-tuple-element.22), channel_id=1, source_target_pairs={{0,2},{2,4},{4,6},{6,8},{8,10},{10,12},{12,14},{14,16},{16,18},{18... | collective-permute-start | bytes 786440 | tf_op jit(solution)/shard_map/ppermute | solution.py:357
  107.3 16.5 %collective-permute-start.5 = (bf16[2,256,256]{2,1,0:T(8,128)(2,1)S(1)}, bf16[2,256,256]{2,1,0:T(8,128)(2,1)S(1)}, u32[]{:S(2)}, u32[]{:S(2)}) collective-permute-start(bf16[2,256,256]{2,1,0:T(8,128)(2,1)S(1)} %collective-permute-done.4), channel_id=1, source_target_pairs={{0,2},{2,4},{4,6},{6,8},{8,10},{10,12},{12,14},{14,16},{16,18},{18... | collective-permute-start | bytes 786440 | tf_op jit(solution)/shard_map/ppermute | solution.py:368
  123.8 11.4 %collective-permute-start.6 = (bf16[2,256,256]{2,1,0:T(8,128)(2,1)S(1)}, bf16[2,256,256]{2,1,0:T(8,128)(2,1)S(1)}, u32[]{:S(2)}, u32[]{:S(2)}) collective-permute-start(bf16[2,256,256]{2,1,0:T(8,128)(2,1)S(1)} %collective-permute-done.5), channel_id=1, source_target_pairs={{0,2},{2,4},{4,6},{6,8},{8,10},{10,12},{12,14},{14,16},{16,18},{18... | collective-permute-start | bytes 786440 | tf_op jit(solution)/shard_map/ppermute | solution.py:378
  135.2 14.6 %collective-permute-start.7 = (bf16[2,256,256]{2,1,0:T(8,128)(2,1)S(1)}, bf16[2,256,256]{2,1,0:T(8,128)(2,1)S(1)}, u32[]{:S(2)}, u32[]{:S(2)}) collective-permute-start(bf16[2,256,256]{2,1,0:T(8,128)(2,1)S(1)} %collective-permute-done.6), channel_id=1, source_target_pairs={{0,2},{2,4},{4,6},{6,8},{8,10},{10,12},{12,14},{14,16},{16,18},{18... | collective-permute-start | bytes 786440 | tf_op jit(solution)/shard_map/ppermute | solution.py:389
  137.2 0.7 copy-start.3
  158.6 19.7 %copy-start.1 = (f32[4096]{0:T(1024)S(1)}, f32[4096]{0:T(1024)}, u32[]{:S(2)}) copy-start(f32[4096]{0:T(1024)} %param.17) | copy-start | bytes 49156

commit v2 on v1

--- a/solution.py
+++ b/solution.py
@@ -174,12 +174,7 @@
 
 def sum_kernel(parts_ref, total_ref):
     total = jnp.sum(parts_ref[...].astype(F32), axis=0, keepdims=True)
-    total_ref[...] = jnp.broadcast_to(total, (8, 96, PART)).astype(BF)
-
-
-def widen_kernel(piece_ref, total_ref):
-    for row in range(4):
-        total_ref[row] = piece_ref[...]
+    total_ref[...] = jnp.broadcast_to(total, (CHIPS, 96, PART)).astype(BF)
 
 
 def whole_weights(slices_ref):
@@ -368,23 +363,15 @@
     chunks.append(lax.ppermute(chunks[-1], RING, ring))
     total = pl.pallas_call(
         sum_kernel,
-        out_shape=shape_of((8, 96, PART)),
+        out_shape=shape_of((CHIPS, 96, PART)),
         in_specs=[VMEM],
         out_specs=VMEM,
         compiler_params=PARAMS,
         name="sum",
     )(parts)
-    total = lax.all_to_all(total, "z", 0, 0, tiled=True)
+    total = lax.all_to_all(total, RING, 0, 0, tiled=True)
+    total = total.reshape(4, 8, 96, PART)
     chunks.append(lax.ppermute(chunks[-1], RING, ring))
-    total = pl.pallas_call(
-        widen_kernel,
-        out_shape=shape_of((4, 8, 96, PART)),
-        in_specs=[VMEM],
-        out_specs=VMEM,
-        compiler_params=PARAMS,
-        name="widen",
-    )(total)
-    total = lax.all_to_all(total, "y_hi", 0, 0, tiled=True)
 
     chunks.append(lax.ppermute(chunks[-1], RING, ring))
     chunks = [chunk.reshape(2, 4, 64, DH) for chunk in chunks]

time: 182 us -> 181 us (level)
  blocking collectives: 61.3 us -> 50.8 us
  waiting for transfers between devices: 65.8 us -> 74.6 us
    ppermute x1, waiting for transfers between devices: 16 us -> 28.6 us  [body(): chunks = [lax.ppermute(context, RING, ring)]]
    all_to_all x1 -> x0, blocking collectives: 11.2 us -> none  [body(): total = lax.all_to_all(total, 'z', 0, 0, tiled=True)]
    ppermute x3, waiting for transfers between devices: 35.5 us -> 31.7 us  [body(): chunks.append(lax.ppermute(chunks[-1], RING, ring))]
where the time goes in v2:
time: 181 us; the launch traced here: 179 us
  waiting for transfers between devices  74.6 us (41%)
  blocking collectives  50.8 us (28%)
  starting transfers between devices  37.3 us (21%)
  Pallas kernels  14.8 us (8%)
    ppermute x3, waiting for transfers between devices, body(): chunks.append(lax.ppermute(chunks[-1], RING, ring))  31.7 us
    ppermute x1, waiting for transfers between devices, body(): chunks = [lax.ppermute(context, RING, ring)]  28.6 us
    all_to_all x1, blocking collectives, body(): gathered = lax.all_to_all(combined, ('core', 'y_lo', 'x'), 0, 0, tiled=True)  20.4 us
    all_to_all x1, blocking collectives, body(): parts = lax.all_to_all(grad, 'z', 0, 0, tiled=True)  15.7 us
    all_to_all x1, blocking collectives, body(): dealt = lax.all_to_all(dealt, 'y_hi', 0, 0, tiled=True)  14.7 us
    ppermute x3, waiting for transfers between devices, body(): lax.ppermute(pool, 'y_hi', [(i, (i + distance) % 4) for i in range(4)])  13 us
    all_to_all x1, starting transfers between devices, body(): dealt = lax.all_to_all(dealt, ('z', 'core'), 0, 0, tiled=True)  13 us
    ppermute x3, starting transfers between devices, body(): lax.ppermute(pool, 'y_hi', [(i, (i + distance) % 4) for i in range(4)])  9.52 us
  transfers between devices with their start and end apart: 10, of which 8 were waited for; matrix products, arithmetic and copies ran while one was open for 0% of the time, Pallas kernels for 1%

profile of v2, /device:TPU:1, one launch (start us, length us, event | category | flops | bytes accessed | tf_op | source)
XLA Modules:
  0.0 178.8 jit_solution(3992970120764364108)
XLA Ops:
  0.0 2.0 %pack.1 = (bf16[392,256]{1,0:T(8,128)(2,1)}, bf16[392,256]{1,0:T(8,128)(2,1)}, bf16[4,48,256]{2,1,0:T(8,128)(2,1)}) custom-call(s32[1]{0:T(128)} %bitcast.1.core_ref, bf16[2,64,512]{2,1,0:T(8,128)(2,1)} %q_in.1, bf16[2,64,512]{2,1,0:T(8,128)(2,1)} %k_in.1, bf16[2,64,512]{2,1,0:T(8,128)(2,1)} %v_in.1, f32[1,2,64]{2,1,0:T(2,128)} %rate_in.1, ...), custom_call_target="tpu_custom_call" | custom-call | tf_op jit(solution)/shard_map/pack/pallas_call | solution.py:319
  2.0 14.7 %all_to_all.25.rows_ref = bf16[4,48,256]{2,1,0:T(8,128)(2,1)S(1)} all-to-all(bf16[4,48,256]{2,1,0:T(8,128)(2,1)} %get-tuple-element.17), channel_id=1, replica_groups=mesh['y_lo'=2,'x'=4,'y_hi'=4,'z'=8,'core'=2] {'y_hi'}, dimensions={0} | all-to-all | bytes 196608 | tf_op jit(solution)/shard_map/all_to_all | solution.py:329
  16.7 0.9 regroup.1
  17.6 13.0 %all-to-all-start.1 = ((bf16[16,96,256]{2,1,0:T(8,128)(2,1)}), bf16[16,96,256]{2,1,0:T(8,128)(2,1)S(1)}, u32[]{:S(2)}, u32[]{:S(2)}) async-start(bf16[16,96,256]{2,1,0:T(8,128)(2,1)} %regroup.1), calls=%async_computation.1 | async-start | bytes 1572864 | tf_op jit(solution)/shard_map/all_to_all | solution.py:338
  30.6 2.0 %collective-permute-start = (bf16[392,256]{1,0:T(8,128)(2,1)S(1)}, bf16[392,256]{1,0:T(8,128)(2,1)S(1)}, u32[]{:S(2)}, u32[]{:S(2)}) collective-permute-start(bf16[392,256]{1,0:T(8,128)(2,1)S(1)} %copy-done.2), channel_id=1, source_target_pairs={{0,1},{1,0},{2,3},{3,2},{4,5},{5,4},{6,7},{7,6},{8,9},{9,8},{10,11... | collective-permute-start | bytes 602120 | tf_op jit(solution)/shard_map/ppermute | solution.py:339
  32.6 1.3 collective-permute-done.arrived_ref
  33.9 0.1 arrange.1
  34.0 2.0 %collective-permute-start.1 = (bf16[272,256]{1,0:T(8,128)(2,1)S(1)}, bf16[272,256]{1,0:T(8,128)(2,1)S(1)}, u32[]{:S(2)}, u32[]{:S(2)}) collective-permute-start(bf16[272,256]{1,0:T(8,128)(2,1)S(1)} %get-tuple-element.16.p0_ref), channel_id=1, source_target_pairs={{0,16},{16,32},{32,48},{48,0},{1,17},{17,33},{33,49},{49,1},{2,18}... | collective-permute-start | bytes 417800 | tf_op jit(solution)/shard_map/ppermute | solution.py:350
  36.0 3.8 %collective-permute-start.2 = (bf16[272,256]{1,0:T(8,128)(2,1)S(1)}, bf16[272,256]{1,0:T(8,128)(2,1)S(1)}, u32[]{:S(2)}, u32[]{:S(2)}) collective-permute-start(bf16[272,256]{1,0:T(8,128)(2,1)S(1)} %get-tuple-element.16.p0_ref), channel_id=1, source_target_pairs={{0,32},{16,48},{32,0},{48,16},{1,33},{17,49},{33,1},{49,17},{2,34}... | collective-permute-start | bytes 417800 | tf_op jit(solution)/shard_map/ppermute | solution.py:350
  39.9 3.6 %collective-permute-start.3 = (bf16[272,256]{1,0:T(8,128)(2,1)S(1)}, bf16[272,256]{1,0:T(8,128)(2,1)S(1)}, u32[]{:S(2)}, u32[]{:S(2)}) collective-permute-start(bf16[272,256]{1,0:T(8,128)(2,1)S(1)} %get-tuple-element.16.p0_ref), channel_id=1, source_target_pairs={{0,48},{16,0},{32,16},{48,32},{1,49},{17,1},{33,17},{49,33},{2,50}... | collective-permute-start | bytes 417800 | tf_op jit(solution)/shard_map/ppermute | solution.py:350
  43.5 1.9 %collective-permute-done.1.p1_ref = bf16[272,256]{1,0:T(8,128)(2,1)S(1)} collective-permute-done((bf16[272,256]{1,0:T(8,128)(2,1)S(1)}, bf16[272,256]{1,0:T(8,128)(2,1)S(1)}, u32[]{:S(2)}, u32[]{:S(2)}) %collective-permute-start.1) | collective-permute-done | bytes 139296 | tf_op jit(solution)/shard_map/ppermute | solution.py:350
  45.4 4.8 %collective-permute-done.2.p2_ref = bf16[272,256]{1,0:T(8,128)(2,1)S(1)} collective-permute-done((bf16[272,256]{1,0:T(8,128)(2,1)S(1)}, bf16[272,256]{1,0:T(8,128)(2,1)S(1)}, u32[]{:S(2)}, u32[]{:S(2)}) %collective-permute-start.2) | collective-permute-done | bytes 139296 | tf_op jit(solution)/shard_map/ppermute | solution.py:350
  50.2 6.3 %collective-permute-done.3.p3_ref = bf16[272,256]{1,0:T(8,128)(2,1)S(1)} collective-permute-done((bf16[272,256]{1,0:T(8,128)(2,1)S(1)}, bf16[272,256]{1,0:T(8,128)(2,1)S(1)}, u32[]{:S(2)}, u32[]{:S(2)}) %collective-permute-start.3) | collective-permute-done | bytes 139296 | tf_op jit(solution)/shard_map/ppermute | solution.py:350
  56.5 1.3 grad.1
  57.8 15.7 %all_to_all.26.parts_ref = bf16[8,96,128]{2,1,0:T(8,128)(2,1)S(1)} all-to-all(bf16[8,96,128]{2,1,0:T(8,128)(2,1)S(1)} %get-tuple-element.18), channel_id=1, replica_groups=mesh['y_lo'=2,'x'=4,'y_hi'=4,'z'=8,'core'=2] {'z'}, dimensions={0} | all-to-all | bytes 393216 | tf_op jit(solution)/shard_map/all_to_all | solution.py:362
  73.5 1.0 sum.1
  74.5 3.9 %all-to-all-start.3 = ((bf16[32,96,128]{2,1,0:T(8,128)(2,1)}), bf16[32,96,128]{2,1,0:T(8,128)(2,1)S(1)}, u32[]{:S(2)}, u32[]{:S(2)}) async-start(bf16[32,96,128]{2,1,0:T(8,128)(2,1)} %sum.1), calls=%async_computation.3 | async-start | bytes 1572864 | tf_op jit(solution)/shard_map/all_to_all | solution.py:372
  78.4 3.1 %collective-permute-start.4 = (bf16[2,256,256]{2,1,0:T(8,128)(2,1)S(1)}, bf16[2,256,256]{2,1,0:T(8,128)(2,1)S(1)}, u32[]{:S(2)}, u32[]{:S(2)}) collective-permute-start(bf16[2,256,256]{2,1,0:T(8,128)(2,1)S(1)} %get-tuple-element.22), channel_id=1, source_target_pairs={{0,2},{2,4},{4,6},{6,8},{8,10},{10,12},{12,14},{14,16},{16,18},{18... | collective-permute-start | bytes 786440 | tf_op jit(solution)/shard_map/ppermute | solution.py:352
  81.5 28.6 %collective-permute-done.4 = bf16[2,256,256]{2,1,0:T(8,128)(2,1)S(1)} collective-permute-done((bf16[2,256,256]{2,1,0:T(8,128)(2,1)S(1)}, bf16[2,256,256]{2,1,0:T(8,128)(2,1)S(1)}, u32[]{:S(2)}, u32[]{:S(2)}) %collective-permute-start.4) | collective-permute-done | bytes 262176 | tf_op jit(solution)/shard_map/ppermute | solution.py:352
  110.1 1.9 %collective-permute-start.5 = (bf16[2,256,256]{2,1,0:T(8,128)(2,1)S(1)}, bf16[2,256,256]{2,1,0:T(8,128)(2,1)S(1)}, u32[]{:S(2)}, u32[]{:S(2)}) collective-permute-start(bf16[2,256,256]{2,1,0:T(8,128)(2,1)S(1)} %collective-permute-done.4), channel_id=1, source_target_pairs={{0,2},{2,4},{4,6},{6,8},{8,10},{10,12},{12,14},{14,16},{16,18},{18... | collective-permute-start | bytes 786440 | tf_op jit(solution)/shard_map/ppermute | solution.py:363
  112.0 12.0 %collective-permute-done.5 = bf16[2,256,256]{2,1,0:T(8,128)(2,1)S(1)} collective-permute-done((bf16[2,256,256]{2,1,0:T(8,128)(2,1)S(1)}, bf16[2,256,256]{2,1,0:T(8,128)(2,1)S(1)}, u32[]{:S(2)}, u32[]{:S(2)}) %collective-permute-start.5) | collective-permute-done | bytes 262176 | tf_op jit(solution)/shard_map/ppermute | solution.py:363
  124.0 1.9 %collective-permute-start.6 = (bf16[2,256,256]{2,1,0:T(8,128)(2,1)S(1)}, bf16[2,256,256]{2,1,0:T(8,128)(2,1)S(1)}, u32[]{:S(2)}, u32[]{:S(2)}) collective-permute-start(bf16[2,256,256]{2,1,0:T(8,128)(2,1)S(1)} %collective-permute-done.5), channel_id=1, source_target_pairs={{0,2},{2,4},{4,6},{6,8},{8,10},{10,12},{12,14},{14,16},{16,18},{18... | collective-permute-start | bytes 786440 | tf_op jit(solution)/shard_map/ppermute | solution.py:374
  125.9 10.2 %collective-permute-done.6 = bf16[2,256,256]{2,1,0:T(8,128)(2,1)S(1)} collective-permute-done((bf16[2,256,256]{2,1,0:T(8,128)(2,1)S(1)}, bf16[2,256,256]{2,1,0:T(8,128)(2,1)S(1)}, u32[]{:S(2)}, u32[]{:S(2)}) %collective-permute-start.6) | collective-permute-done | bytes 262176 | tf_op jit(solution)/shard_map/ppermute | solution.py:374
  136.1 1.9 %collective-permute-start.7 = (bf16[2,256,256]{2,1,0:T(8,128)(2,1)S(1)}, bf16[2,256,256]{2,1,0:T(8,128)(2,1)S(1)}, u32[]{:S(2)}, u32[]{:S(2)}) collective-permute-start(bf16[2,256,256]{2,1,0:T(8,128)(2,1)S(1)} %collective-permute-done.6), channel_id=1, source_target_pairs={{0,2},{2,4},{4,6},{6,8},{8,10},{10,12},{12,14},{14,16},{16,18},{18... | collective-permute-start | bytes 786440 | tf_op jit(solution)/shard_map/ppermute | solution.py:376
  138.0 0.0 copy-start.3
  138.1 0.6 copy-done.3
  138.7 0.6 dynamic_slice.3.step_ref
  139.3 9.5 %collective-permute-done.7 = bf16[2,256,256]{2,1,0:T(8,128)(2,1)S(1)} collective-permute-done((bf16[2,256,256]{2,1,0:T(8,128)(2,1)S(1)}, bf16[2,256,256]{2,1,0:T(8,128)(2,1)S(1)}, u32[]{:S(2)}, u32[]{:S(2)}) %collective-permute-start.7) | collective-permute-done | bytes 262176 | tf_op jit(solution)/shard_map/ppermute | solution.py:376
  148.8 1.3 window.1.base_ref
  150.1 7.5 %newton.1 = bf16[16,2,8,256]{3,2,1,0:T(8,128)(2,1)S(1)} custom-call(f32[1]{0:T(128)} %dynamic_slice.3.step_ref, bf16[4,8,96,128]{3,2,1,0:T(8,128)(2,1)S(1)} %bitcast.9, bf16[4,512,128]{2,1,0:T(8,128)(2,1)S(1)} %get-tuple-element.19.slices_ref, bf16[512,256]{1,0:T(8,128)(2,1)S(1)} %get-tuple-element.20.down_ref, ...), custom_call_target="tpu_custom_call" | custom-call | tf_op jit(solution)/shard_map/newton/pallas_call | solution.py:387
  157.6 20.4 %all_to_all.27.parts_ref = bf16[16,2,8,256]{3,2,1,0:T(8,128)(2,1)S(1)} all-to-all(bf16[16,2,8,256]{3,2,1,0:T(8,128)(2,1)S(1)} %newton.1), channel_id=1, replica_groups=mesh['y_lo'=2,'x'=4,'y_hi'=4,'z'=8,'core'=2] {'core','y_lo','x'}, dimensions={0} | all-to-all | bytes 262144 | tf_op jit(solution)/shard_map/all_to_all | solution.py:396
  178.0 0.8 norm.1
  (8 shorter events, 0.0 us)
Async XLA Ops:
  17.6 13.0 %copy-start.2 = (bf16[392,256]{1,0:T(8,128)(2,1)S(1)}, bf16[392,256]{1,0:T(8,128)(2,1)}, u32[]{:S(2)}) copy-start(bf16[392,256]{1,0:T(8,128)(2,1)} %get-tuple-element.15) | copy-start | bytes 602116
  17.6 16.3 %copy-start = (bf16[392,256]{1,0:T(8,128)(2,1)S(1)}, bf16[392,256]{1,0:T(8,128)(2,1)}, u32[]{:S(2)}) copy-start(bf16[392,256]{1,0:T(8,128)(2,1)} %get-tuple-element.14.mine_ref) | copy-start | bytes 602116
  17.6 38.9 %all-to-all-start.1 = ((bf16[16,96,256]{2,1,0:T(8,128)(2,1)}), bf16[16,96,256]{2,1,0:T(8,128)(2,1)S(1)}, u32[]{:S(2)}, u32[]{:S(2)}) async-start(bf16[16,96,256]{2,1,0:T(8,128)(2,1)} %regroup.1), calls=%async_computation.1 | async-start | bytes 1572864 | tf_op jit(solution)/shard_map/all_to_all | solution.py:338
  30.6 3.3 %collective-permute-start = (bf16[392,256]{1,0:T(8,128)(2,1)S(1)}, bf16[392,256]{1,0:T(8,128)(2,1)S(1)}, u32[]{:S(2)}, u32[]{:S(2)}) collective-permute-start(bf16[392,256]{1,0:T(8,128)(2,1)S(1)} %copy-done.2), channel_id=1, source_target_pairs={{0,1},{1,0},{2,3},{3,2},{4,5},{5,4},{6,7},{7,6},{8,9},{9,8},{10,11... | collective-permute-start | bytes 602120 | tf_op jit(solution)/shard_map/ppermute | solution.py:339
  34.0 11.4 %collective-permute-start.1 = (bf16[272,256]{1,0:T(8,128)(2,1)S(1)}, bf16[272,256]{1,0:T(8,128)(2,1)S(1)}, u32[]{:S(2)}, u32[]{:S(2)}) collective-permute-start(bf16[272,256]{1,0:T(8,128)(2,1)S(1)} %get-tuple-element.16.p0_ref), channel_id=1, source_target_pairs={{0,16},{16,32},{32,48},{48,0},{1,17},{17,33},{33,49},{49,1},{2,18}... | collective-permute-start | bytes 417800 | tf_op jit(solution)/shard_map/ppermute | solution.py:350
  36.0 14.2 %collective-permute-start.2 = (bf16[272,256]{1,0:T(8,128)(2,1)S(1)}, bf16[272,256]{1,0:T(8,128)(2,1)S(1)}, u32[]{:S(2)}, u32[]{:S(2)}) collective-permute-start(bf16[272,256]{1,0:T(8,128)(2,1)S(1)} %get-tuple-element.16.p0_ref), channel_id=1, source_target_pairs={{0,32},{16,48},{32,0},{48,16},{1,33},{17,49},{33,1},{49,17},{2,34}... | collective-permute-start | bytes 417800 | tf_op jit(solution)/shard_map/ppermute | solution.py:350
  39.9 16.7 %collective-permute-start.3 = (bf16[272,256]{1,0:T(8,128)(2,1)S(1)}, bf16[272,256]{1,0:T(8,128)(2,1)S(1)}, u32[]{:S(2)}, u32[]{:S(2)}) collective-permute-start(bf16[272,256]{1,0:T(8,128)(2,1)S(1)} %get-tuple-element.16.p0_ref), channel_id=1, source_target_pairs={{0,48},{16,0},{32,16},{48,32},{1,49},{17,1},{33,17},{49,33},{2,50}... | collective-permute-start | bytes 417800 | tf_op jit(solution)/shard_map/ppermute | solution.py:350
  74.5 75.6 %all-to-all-start.3 = ((bf16[32,96,128]{2,1,0:T(8,128)(2,1)}), bf16[32,96,128]{2,1,0:T(8,128)(2,1)S(1)}, u32[]{:S(2)}, u32[]{:S(2)}) async-start(bf16[32,96,128]{2,1,0:T(8,128)(2,1)} %sum.1), calls=%async_computation.3 | async-start | bytes 1572864 | tf_op jit(solution)/shard_map/all_to_all | solution.py:372
  78.4 31.7 %collective-permute-start.4 = (bf16[2,256,256]{2,1,0:T(8,128)(2,1)S(1)}, bf16[2,256,256]{2,1,0:T(8,128)(2,1)S(1)}, u32[]{:S(2)}, u32[]{:S(2)}) collective-permute-start(bf16[2,256,256]{2,1,0:T(8,128)(2,1)S(1)} %get-tuple-element.22), channel_id=1, source_target_pairs={{0,2},{2,4},{4,6},{6,8},{8,10},{10,12},{12,14},{14,16},{16,18},{18... | collective-permute-start | bytes 786440 | tf_op jit(solution)/shard_map/ppermute | solution.py:352
  110.1 13.9 %collective-permute-start.5 = (bf16[2,256,256]{2,1,0:T(8,128)(2,1)S(1)}, bf16[2,256,256]{2,1,0:T(8,128)(2,1)S(1)}, u32[]{:S(2)}, u32[]{:S(2)}) collective-permute-start(bf16[2,256,256]{2,1,0:T(8,128)(2,1)S(1)} %collective-permute-done.4), channel_id=1, source_target_pairs={{0,2},{2,4},{4,6},{6,8},{8,10},{10,12},{12,14},{14,16},{16,18},{18... | collective-permute-start | bytes 786440 | tf_op jit(solution)/shard_map/ppermute | solution.py:363
  124.0 12.1 %collective-permute-start.6 = (bf16[2,256,256]{2,1,0:T(8,128)(2,1)S(1)}, bf16[2,256,256]{2,1,0:T(8,128)(2,1)S(1)}, u32[]{:S(2)}, u32[]{:S(2)}) collective-permute-start(bf16[2,256,256]{2,1,0:T(8,128)(2,1)S(1)} %collective-permute-done.5), channel_id=1, source_target_pairs={{0,2},{2,4},{4,6},{6,8},{8,10},{10,12},{12,14},{14,16},{16,18},{18... | collective-permute-start | bytes 786440 | tf_op jit(solution)/shard_map/ppermute | solution.py:374
  136.1 12.7 %collective-permute-start.7 = (bf16[2,256,256]{2,1,0:T(8,128)(2,1)S(1)}, bf16[2,256,256]{2,1,0:T(8,128)(2,1)S(1)}, u32[]{:S(2)}, u32[]{:S(2)}) collective-permute-start(bf16[2,256,256]{2,1,0:T(8,128)(2,1)S(1)} %collective-permute-done.6), channel_id=1, source_target_pairs={{0,2},{2,4},{4,6},{6,8},{8,10},{10,12},{12,14},{14,16},{16,18},{18... | collective-permute-start | bytes 786440 | tf_op jit(solution)/shard_map/ppermute | solution.py:376
  138.0 0.7 copy-start.3
  157.6 20.4 %copy-start.1 = (f32[4096]{0:T(1024)S(1)}, f32[4096]{0:T(1024)}, u32[]{:S(2)}) copy-start(f32[4096]{0:T(1024)} %param.17) | copy-start | bytes 49156

commit v3 on v0

--- a/solution.py
+++ b/solution.py
@@ -174,12 +174,7 @@
 
 def sum_kernel(parts_ref, total_ref):
     total = jnp.sum(parts_ref[...].astype(F32), axis=0, keepdims=True)
-    total_ref[...] = jnp.broadcast_to(total, (8, 96, PART)).astype(BF)
-
-
-def widen_kernel(piece_ref, total_ref):
-    for row in range(4):
-        total_ref[row] = piece_ref[...]
+    total_ref[...] = jnp.broadcast_to(total, (CHIPS, 96, PART)).astype(BF)
 
 
 def whole_weights(slices_ref):
@@ -368,23 +363,15 @@
     chunks.append(lax.ppermute(chunks[-1], RING, ring))
     total = pl.pallas_call(
         sum_kernel,
-        out_shape=shape_of((8, 96, PART)),
+        out_shape=shape_of((CHIPS, 96, PART)),
         in_specs=[VMEM],
         out_specs=VMEM,
         compiler_params=PARAMS,
         name="sum",
     )(parts)
-    total = lax.all_to_all(total, "z", 0, 0, tiled=True)
     chunks.append(lax.ppermute(chunks[-1], RING, ring))
-    total = pl.pallas_call(
-        widen_kernel,
-        out_shape=shape_of((4, 8, 96, PART)),
-        in_specs=[VMEM],
-        out_specs=VMEM,
-        compiler_params=PARAMS,
-        name="widen",
-    )(total)
-    total = lax.all_to_all(total, "y_hi", 0, 0, tiled=True)
+    total = lax.all_to_all(total, RING, 0, 0, tiled=True)
+    total = total.reshape(4, 8, 96, PART)
 
     step = lax.dynamic_slice_in_dim(step_size, core, 1, 0)
     fast = pl.pallas_call(

time: 174 us -> 174 us (level)
  blocking collectives: 61.3 us -> 50.8 us
  waiting for transfers between devices: 58.3 us -> 67.1 us
    ppermute x1, waiting for transfers between devices: 16 us -> 28.6 us  [body(): chunks = [lax.ppermute(context, RING, ring)]]
    all_to_all x1 -> x0, blocking collectives: 11.2 us -> none  [body(): total = lax.all_to_all(total, 'z', 0, 0, tiled=True)]
    ppermute x3, waiting for transfers between devices: 28 us -> 24.2 us  [body(): chunks.append(lax.ppermute(chunks[-1], RING, ring))]
where the time goes in v3:
time: 174 us; the launch traced here: 171 us
  waiting for transfers between devices  67.1 us (39%)
  blocking collectives  50.8 us (29%)
  starting transfers between devices  37.3 us (21%)
  Pallas kernels  14.8 us (9%)
    ppermute x1, waiting for transfers between devices, body(): chunks = [lax.ppermute(context, RING, ring)]  28.6 us
    ppermute x3, waiting for transfers between devices, body(): chunks.append(lax.ppermute(chunks[-1], RING, ring))  24.2 us
    all_to_all x1, blocking collectives, body(): gathered = lax.all_to_all(combined, ('core', 'y_lo', 'x'), 0, 0, tiled=True)  20.4 us
    all_to_all x1, blocking collectives, body(): parts = lax.all_to_all(grad, 'z', 0, 0, tiled=True)  15.7 us
    all_to_all x1, blocking collectives, body(): dealt = lax.all_to_all(dealt, 'y_hi', 0, 0, tiled=True)  14.7 us
    ppermute x3, waiting for transfers between devices, body(): lax.ppermute(pool, 'y_hi', [(i, (i + distance) % 4) for i in range(4)])  13 us
    all_to_all x1, starting transfers between devices, body(): dealt = lax.all_to_all(dealt, ('z', 'core'), 0, 0, tiled=True)  13 us
    ppermute x3, starting transfers between devices, body(): lax.ppermute(pool, 'y_hi', [(i, (i + distance) % 4) for i in range(4)])  9.52 us
  transfers between devices with their start and end apart: 10, of which 8 were waited for; matrix products, arithmetic and copies ran while one was open for 0% of the time, Pallas kernels for 4%

profile of v3, /device:TPU:1, one launch (start us, length us, event | category | flops | bytes accessed | tf_op | source)
XLA Modules:
  0.0 171.3 jit_solution(6167706243410419154)
XLA Ops:
  0.0 2.0 %pack.1 = (bf16[392,256]{1,0:T(8,128)(2,1)}, bf16[392,256]{1,0:T(8,128)(2,1)}, bf16[4,48,256]{2,1,0:T(8,128)(2,1)}) custom-call(s32[1]{0:T(128)} %bitcast.1.core_ref, bf16[2,64,512]{2,1,0:T(8,128)(2,1)} %q_in.1, bf16[2,64,512]{2,1,0:T(8,128)(2,1)} %k_in.1, bf16[2,64,512]{2,1,0:T(8,128)(2,1)} %v_in.1, f32[1,2,64]{2,1,0:T(2,128)} %rate_in.1, ...), custom_call_target="tpu_custom_call" | custom-call | tf_op jit(solution)/shard_map/pack/pallas_call | solution.py:319
  2.0 14.7 %all_to_all.25.rows_ref = bf16[4,48,256]{2,1,0:T(8,128)(2,1)S(1)} all-to-all(bf16[4,48,256]{2,1,0:T(8,128)(2,1)} %get-tuple-element.19), channel_id=1, replica_groups=mesh['y_lo'=2,'x'=4,'y_hi'=4,'z'=8,'core'=2] {'y_hi'}, dimensions={0} | all-to-all | bytes 196608 | tf_op jit(solution)/shard_map/all_to_all | solution.py:329
  16.7 0.9 regroup.1
  17.6 13.0 %all-to-all-start.1 = ((bf16[16,96,256]{2,1,0:T(8,128)(2,1)}), bf16[16,96,256]{2,1,0:T(8,128)(2,1)S(1)}, u32[]{:S(2)}, u32[]{:S(2)}) async-start(bf16[16,96,256]{2,1,0:T(8,128)(2,1)} %regroup.1), calls=%async_computation.1 | async-start | bytes 1572864 | tf_op jit(solution)/shard_map/all_to_all | solution.py:338
  30.6 2.0 %collective-permute-start = (bf16[392,256]{1,0:T(8,128)(2,1)S(1)}, bf16[392,256]{1,0:T(8,128)(2,1)S(1)}, u32[]{:S(2)}, u32[]{:S(2)}) collective-permute-start(bf16[392,256]{1,0:T(8,128)(2,1)S(1)} %copy-done.2), channel_id=1, source_target_pairs={{0,1},{1,0},{2,3},{3,2},{4,5},{5,4},{6,7},{7,6},{8,9},{9,8},{10,11... | collective-permute-start | bytes 602120 | tf_op jit(solution)/shard_map/ppermute | solution.py:339
  32.6 1.3 collective-permute-done.arrived_ref
  33.9 0.1 arrange.1
  34.0 2.0 %collective-permute-start.5 = (bf16[272,256]{1,0:T(8,128)(2,1)S(1)}, bf16[272,256]{1,0:T(8,128)(2,1)S(1)}, u32[]{:S(2)}, u32[]{:S(2)}) collective-permute-start(bf16[272,256]{1,0:T(8,128)(2,1)S(1)} %get-tuple-element.18.p0_ref), channel_id=1, source_target_pairs={{0,16},{16,32},{32,48},{48,0},{1,17},{17,33},{33,49},{49,1},{2,18}... | collective-permute-start | bytes 417800 | tf_op jit(solution)/shard_map/ppermute | solution.py:350
  36.0 3.8 %collective-permute-start.6 = (bf16[272,256]{1,0:T(8,128)(2,1)S(1)}, bf16[272,256]{1,0:T(8,128)(2,1)S(1)}, u32[]{:S(2)}, u32[]{:S(2)}) collective-permute-start(bf16[272,256]{1,0:T(8,128)(2,1)S(1)} %get-tuple-element.18.p0_ref), channel_id=1, source_target_pairs={{0,32},{16,48},{32,0},{48,16},{1,33},{17,49},{33,1},{49,17},{2,34}... | collective-permute-start | bytes 417800 | tf_op jit(solution)/shard_map/ppermute | solution.py:350
  39.9 3.6 %collective-permute-start.7 = (bf16[272,256]{1,0:T(8,128)(2,1)S(1)}, bf16[272,256]{1,0:T(8,128)(2,1)S(1)}, u32[]{:S(2)}, u32[]{:S(2)}) collective-permute-start(bf16[272,256]{1,0:T(8,128)(2,1)S(1)} %get-tuple-element.18.p0_ref), channel_id=1, source_target_pairs={{0,48},{16,0},{32,16},{48,32},{1,49},{17,1},{33,17},{49,33},{2,50}... | collective-permute-start | bytes 417800 | tf_op jit(solution)/shard_map/ppermute | solution.py:350
  43.5 1.9 %collective-permute-done.5.p1_ref = bf16[272,256]{1,0:T(8,128)(2,1)S(1)} collective-permute-done((bf16[272,256]{1,0:T(8,128)(2,1)S(1)}, bf16[272,256]{1,0:T(8,128)(2,1)S(1)}, u32[]{:S(2)}, u32[]{:S(2)}) %collective-permute-start.5) | collective-permute-done | bytes 139296 | tf_op jit(solution)/shard_map/ppermute | solution.py:350
  45.4 4.8 %collective-permute-done.6.p2_ref = bf16[272,256]{1,0:T(8,128)(2,1)S(1)} collective-permute-done((bf16[272,256]{1,0:T(8,128)(2,1)S(1)}, bf16[272,256]{1,0:T(8,128)(2,1)S(1)}, u32[]{:S(2)}, u32[]{:S(2)}) %collective-permute-start.6) | collective-permute-done | bytes 139296 | tf_op jit(solution)/shard_map/ppermute | solution.py:350
  50.2 6.3 %collective-permute-done.7.p3_ref = bf16[272,256]{1,0:T(8,128)(2,1)S(1)} collective-permute-done((bf16[272,256]{1,0:T(8,128)(2,1)S(1)}, bf16[272,256]{1,0:T(8,128)(2,1)S(1)}, u32[]{:S(2)}, u32[]{:S(2)}) %collective-permute-start.7) | collective-permute-done | bytes 139296 | tf_op jit(solution)/shard_map/ppermute | solution.py:350
  56.5 1.3 grad.1
  57.8 15.7 %all_to_all.26.parts_ref = bf16[8,96,128]{2,1,0:T(8,128)(2,1)S(1)} all-to-all(bf16[8,96,128]{2,1,0:T(8,128)(2,1)S(1)} %get-tuple-element.22), channel_id=1, replica_groups=mesh['y_lo'=2,'x'=4,'y_hi'=4,'z'=8,'core'=2] {'z'}, dimensions={0} | all-to-all | bytes 393216 | tf_op jit(solution)/shard_map/all_to_all | solution.py:362
  73.5 1.0 sum.1
  74.5 3.9 %all-to-all-start.3 = ((bf16[32,96,128]{2,1,0:T(8,128)(2,1)}), bf16[32,96,128]{2,1,0:T(8,128)(2,1)S(1)}, u32[]{:S(2)}, u32[]{:S(2)}) async-start(bf16[32,96,128]{2,1,0:T(8,128)(2,1)} %sum.1), calls=%async_computation.3 | async-start | bytes 1572864 | tf_op jit(solution)/shard_map/all_to_all | solution.py:373
  78.4 3.1 %collective-permute-start.1 = (bf16[2,256,256]{2,1,0:T(8,128)(2,1)S(1)}, bf16[2,256,256]{2,1,0:T(8,128)(2,1)S(1)}, u32[]{:S(2)}, u32[]{:S(2)}) collective-permute-start(bf16[2,256,256]{2,1,0:T(8,128)(2,1)S(1)} %get-tuple-element.17), channel_id=1, source_target_pairs={{0,2},{2,4},{4,6},{6,8},{8,10},{10,12},{12,14},{14,16},{16,18},{18... | collective-permute-start | bytes 786440 | tf_op jit(solution)/shard_map/ppermute | solution.py:352
  81.5 28.6 %collective-permute-done.1 = bf16[2,256,256]{2,1,0:T(8,128)(2,1)S(1)} collective-permute-done((bf16[2,256,256]{2,1,0:T(8,128)(2,1)S(1)}, bf16[2,256,256]{2,1,0:T(8,128)(2,1)S(1)}, u32[]{:S(2)}, u32[]{:S(2)}) %collective-permute-start.1) | collective-permute-done | bytes 262176 | tf_op jit(solution)/shard_map/ppermute | solution.py:352
  110.1 1.9 %collective-permute-start.2 = (bf16[2,256,256]{2,1,0:T(8,128)(2,1)S(1)}, bf16[2,256,256]{2,1,0:T(8,128)(2,1)S(1)}, u32[]{:S(2)}, u32[]{:S(2)}) collective-permute-start(bf16[2,256,256]{2,1,0:T(8,128)(2,1)S(1)} %collective-permute-done.1), channel_id=1, source_target_pairs={{0,2},{2,4},{4,6},{6,8},{8,10},{10,12},{12,14},{14,16},{16,18},{18... | collective-permute-start | bytes 786440 | tf_op jit(solution)/shard_map/ppermute | solution.py:363
  112.0 12.0 %collective-permute-done.2 = bf16[2,256,256]{2,1,0:T(8,128)(2,1)S(1)} collective-permute-done((bf16[2,256,256]{2,1,0:T(8,128)(2,1)S(1)}, bf16[2,256,256]{2,1,0:T(8,128)(2,1)S(1)}, u32[]{:S(2)}, u32[]{:S(2)}) %collective-permute-start.2) | collective-permute-done | bytes 262176 | tf_op jit(solution)/shard_map/ppermute | solution.py:363
  124.0 1.9 %collective-permute-start.3 = (bf16[2,256,256]{2,1,0:T(8,128)(2,1)S(1)}, bf16[2,256,256]{2,1,0:T(8,128)(2,1)S(1)}, u32[]{:S(2)}, u32[]{:S(2)}) collective-permute-start(bf16[2,256,256]{2,1,0:T(8,128)(2,1)S(1)} %collective-permute-done.2), channel_id=1, source_target_pairs={{0,2},{2,4},{4,6},{6,8},{8,10},{10,12},{12,14},{14,16},{16,18},{18... | collective-permute-start | bytes 786440 | tf_op jit(solution)/shard_map/ppermute | solution.py:372
  125.9 0.0 copy-start.3
  125.9 0.6 copy-done.3
  126.6 0.6 dynamic_slice.3.step_ref
  127.2 8.9 %collective-permute-done.3._ = bf16[2,256,256]{2,1,0:T(8,128)(2,1)S(1)} collective-permute-done((bf16[2,256,256]{2,1,0:T(8,128)(2,1)S(1)}, bf16[2,256,256]{2,1,0:T(8,128)(2,1)S(1)}, u32[]{:S(2)}, u32[]{:S(2)}) %collective-permute-start.3) | collective-permute-done | bytes 262176 | tf_op jit(solution)/shard_map/ppermute | solution.py:372
  136.1 1.9 %collective-permute-start.4 = (bf16[2,256,256]{2,1,0:T(8,128)(2,1)S(1)}, bf16[2,256,256]{2,1,0:T(8,128)(2,1)S(1)}, u32[]{:S(2)}, u32[]{:S(2)}) collective-permute-start(bf16[2,256,256]{2,1,0:T(8,128)(2,1)S(1)} %collective-permute-done.3._), channel_id=1, source_target_pairs={{0,2},{2,4},{4,6},{6,8},{8,10},{10,12},{12,14},{14,16},{16,18},{18... | collective-permute-start | bytes 786440 | tf_op jit(solution)/shard_map/ppermute | solution.py:389
  138.0 7.4 %newton.1.fast_ref = f32[128,256]{1,0:T(8,128)S(1)} custom-call(f32[1]{0:T(128)} %dynamic_slice.3.step_ref, bf16[4,8,96,128]{3,2,1,0:T(8,128)(2,1)S(1)} %bitcast.9, bf16[4,512,128]{2,1,0:T(8,128)(2,1)S(1)} %get-tuple-element.20.slices_ref, bf16[512,256]{1,0:T(8,128)(2,1)S(1)} %get-tuple-element.21.down_ref, ...), custom_call_target="tpu_custom_call" | custom-call | flops 8000000000 | bytes 4000000 | tf_op jit(solution)/shard_map/newton/pallas_call | solution.py:377
  145.5 3.3 %collective-permute-done.4 = bf16[2,256,256]{2,1,0:T(8,128)(2,1)S(1)} collective-permute-done((bf16[2,256,256]{2,1,0:T(8,128)(2,1)S(1)}, bf16[2,256,256]{2,1,0:T(8,128)(2,1)S(1)}, u32[]{:S(2)}, u32[]{:S(2)}) %collective-permute-start.4) | collective-permute-done | bytes 262176 | tf_op jit(solution)/shard_map/ppermute | solution.py:389
  148.8 1.3 window.1
  150.1 20.4 %all_to_all.27.parts_ref = bf16[16,2,8,256]{3,2,1,0:T(8,128)(2,1)S(1)} all-to-all(bf16[16,2,8,256]{3,2,1,0:T(8,128)(2,1)S(1)} %window.1), channel_id=1, replica_groups=mesh['y_lo'=2,'x'=4,'y_hi'=4,'z'=8,'core'=2] {'core','y_lo','x'}, dimensions={0} | all-to-all | bytes 262144 | tf_op jit(solution)/shard_map/all_to_all | solution.py:399
  170.5 0.8 norm.1
  (8 shorter events, 0.0 us)
Async XLA Ops:
  17.6 13.0 %copy-start.2 = (bf16[392,256]{1,0:T(8,128)(2,1)S(1)}, bf16[392,256]{1,0:T(8,128)(2,1)}, u32[]{:S(2)}) copy-start(bf16[392,256]{1,0:T(8,128)(2,1)} %get-tuple-element.15) | copy-start | bytes 602116
  17.6 16.3 %copy-start = (bf16[392,256]{1,0:T(8,128)(2,1)S(1)}, bf16[392,256]{1,0:T(8,128)(2,1)}, u32[]{:S(2)}) copy-start(bf16[392,256]{1,0:T(8,128)(2,1)} %get-tuple-element.14.mine_ref) | copy-start | bytes 602116
  17.6 38.9 %all-to-all-start.1 = ((bf16[16,96,256]{2,1,0:T(8,128)(2,1)}), bf16[16,96,256]{2,1,0:T(8,128)(2,1)S(1)}, u32[]{:S(2)}, u32[]{:S(2)}) async-start(bf16[16,96,256]{2,1,0:T(8,128)(2,1)} %regroup.1), calls=%async_computation.1 | async-start | bytes 1572864 | tf_op jit(solution)/shard_map/all_to_all | solution.py:338
  30.6 3.3 %collective-permute-start = (bf16[392,256]{1,0:T(8,128)(2,1)S(1)}, bf16[392,256]{1,0:T(8,128)(2,1)S(1)}, u32[]{:S(2)}, u32[]{:S(2)}) collective-permute-start(bf16[392,256]{1,0:T(8,128)(2,1)S(1)} %copy-done.2), channel_id=1, source_target_pairs={{0,1},{1,0},{2,3},{3,2},{4,5},{5,4},{6,7},{7,6},{8,9},{9,8},{10,11... | collective-permute-start | bytes 602120 | tf_op jit(solution)/shard_map/ppermute | solution.py:339
  34.0 11.4 %collective-permute-start.5 = (bf16[272,256]{1,0:T(8,128)(2,1)S(1)}, bf16[272,256]{1,0:T(8,128)(2,1)S(1)}, u32[]{:S(2)}, u32[]{:S(2)}) collective-permute-start(bf16[272,256]{1,0:T(8,128)(2,1)S(1)} %get-tuple-element.18.p0_ref), channel_id=1, source_target_pairs={{0,16},{16,32},{32,48},{48,0},{1,17},{17,33},{33,49},{49,1},{2,18}... | collective-permute-start | bytes 417800 | tf_op jit(solution)/shard_map/ppermute | solution.py:350
  36.0 14.2 %collective-permute-start.6 = (bf16[272,256]{1,0:T(8,128)(2,1)S(1)}, bf16[272,256]{1,0:T(8,128)(2,1)S(1)}, u32[]{:S(2)}, u32[]{:S(2)}) collective-permute-start(bf16[272,256]{1,0:T(8,128)(2,1)S(1)} %get-tuple-element.18.p0_ref), channel_id=1, source_target_pairs={{0,32},{16,48},{32,0},{48,16},{1,33},{17,49},{33,1},{49,17},{2,34}... | collective-permute-start | bytes 417800 | tf_op jit(solution)/shard_map/ppermute | solution.py:350
  39.9 16.7 %collective-permute-start.7 = (bf16[272,256]{1,0:T(8,128)(2,1)S(1)}, bf16[272,256]{1,0:T(8,128)(2,1)S(1)}, u32[]{:S(2)}, u32[]{:S(2)}) collective-permute-start(bf16[272,256]{1,0:T(8,128)(2,1)S(1)} %get-tuple-element.18.p0_ref), channel_id=1, source_target_pairs={{0,48},{16,0},{32,16},{48,32},{1,49},{17,1},{33,17},{49,33},{2,50}... | collective-permute-start | bytes 417800 | tf_op jit(solution)/shard_map/ppermute | solution.py:350
  74.5 63.6 %all-to-all-start.3 = ((bf16[32,96,128]{2,1,0:T(8,128)(2,1)}), bf16[32,96,128]{2,1,0:T(8,128)(2,1)S(1)}, u32[]{:S(2)}, u32[]{:S(2)}) async-start(bf16[32,96,128]{2,1,0:T(8,128)(2,1)} %sum.1), calls=%async_computation.3 | async-start | bytes 1572864 | tf_op jit(solution)/shard_map/all_to_all | solution.py:373
  78.4 31.7 %collective-permute-start.1 = (bf16[2,256,256]{2,1,0:T(8,128)(2,1)S(1)}, bf16[2,256,256]{2,1,0:T(8,128)(2,1)S(1)}, u32[]{:S(2)}, u32[]{:S(2)}) collective-permute-start(bf16[2,256,256]{2,1,0:T(8,128)(2,1)S(1)} %get-tuple-element.17), channel_id=1, source_target_pairs={{0,2},{2,4},{4,6},{6,8},{8,10},{10,12},{12,14},{14,16},{16,18},{18... | collective-permute-start | bytes 786440 | tf_op jit(solution)/shard_map/ppermute | solution.py:352
  110.1 13.9 %collective-permute-start.2 = (bf16[2,256,256]{2,1,0:T(8,128)(2,1)S(1)}, bf16[2,256,256]{2,1,0:T(8,128)(2,1)S(1)}, u32[]{:S(2)}, u32[]{:S(2)}) collective-permute-start(bf16[2,256,256]{2,1,0:T(8,128)(2,1)S(1)} %collective-permute-done.1), channel_id=1, source_target_pairs={{0,2},{2,4},{4,6},{6,8},{8,10},{10,12},{12,14},{14,16},{16,18},{18... | collective-permute-start | bytes 786440 | tf_op jit(solution)/shard_map/ppermute | solution.py:363
  124.0 12.1 %collective-permute-start.3 = (bf16[2,256,256]{2,1,0:T(8,128)(2,1)S(1)}, bf16[2,256,256]{2,1,0:T(8,128)(2,1)S(1)}, u32[]{:S(2)}, u32[]{:S(2)}) collective-permute-start(bf16[2,256,256]{2,1,0:T(8,128)(2,1)S(1)} %collective-permute-done.2), channel_id=1, source_target_pairs={{0,2},{2,4},{4,6},{6,8},{8,10},{10,12},{12,14},{14,16},{16,18},{18... | collective-permute-start | bytes 786440 | tf_op jit(solution)/shard_map/ppermute | solution.py:372
  125.9 0.7 copy-start.3
  136.1 12.7 %collective-permute-start.4 = (bf16[2,256,256]{2,1,0:T(8,128)(2,1)S(1)}, bf16[2,256,256]{2,1,0:T(8,128)(2,1)S(1)}, u32[]{:S(2)}, u32[]{:S(2)}) collective-permute-start(bf16[2,256,256]{2,1,0:T(8,128)(2,1)S(1)} %collective-permute-done.3._), channel_id=1, source_target_pairs={{0,2},{2,4},{4,6},{6,8},{8,10},{10,12},{12,14},{14,16},{16,18},{18... | collective-permute-start | bytes 786440 | tf_op jit(solution)/shard_map/ppermute | solution.py:389
  150.1 20.4 %copy-start.1 = (f32[4096]{0:T(1024)S(1)}, f32[4096]{0:T(1024)}, u32[]{:S(2)}) copy-start(f32[4096]{0:T(1024)} %param.17) | copy-start | bytes 49156
